TPU v7x, 256 devices: a whole 4x4x8 slice. The times are simulated.
256 devices in a mesh: tm: 8 (over y_lo, x), tok: 32 (over y_hi, z, core).
Axes of the slice: x: 4, y: 4 (y_hi: 2, y_lo: 2; y = y_hi * 2 + y_lo), z: 8, core: 2. Of those that a mesh axis runs over, the one named last changes fastest.
Arguments:
- start: bfloat16 [4096, 1536], P('tok'), may hold values from -6 to 6
- trajectory: bfloat16 [16, 4096, 1536], P('tm', 'tok'), may hold values from -6 to 6
- plan: int32 [17], replicated, may hold values from 0 to 1000, as said below
- neighbors: int32 [64, 3], P('tok'), may hold values from 0 to 63, as said below
- mod_weight: bfloat16 [256, 3072], replicated, may hold values from -0.75 to 0.75
- w_qkv: bfloat16 [1536, 4608], P('tok'), may hold values from -0.15625 to 0.15625
- w_out: bfloat16 [1536, 1536], P('tok'), may hold values from -1.25 to 1.25
Outputs:
- updated: float32 [16, 4096, 1536], P('tm', 'tok')
Inputs may be any that keep to these rules, and one draw needn't show every extreme that they name: `plan`: strictly decreasing from 1000 at the first entry to 0 at the last. `neighbors`: entry 0 of row c is c; the other entries lie within 2 of c.
All inputs are finite; a program needn't handle non-finite values.
Results may differ from a plain program's by a relative error of at most 0.0045.
Values may be sent and summed in bfloat16 or wider, within the bound.
A program may use at most 128 MiB of HBM per device.

v0:
```python
import math

import jax
import jax.numpy as jnp
from jax import lax
from jax.sharding import PartitionSpec as P

HEADS = 12
HEAD_DIM = 128
NSCHED = 1000
NB = 3


def padded(block, sides, width):
    for axis, dim in sides:
        count = lax.axis_size(axis)
        forward = [(i, i + 1) for i in range(count - 1)]
        backward = [(target, source) for source, target in forward]
        low = lax.ppermute(
            lax.slice_in_dim(block, block.shape[dim] - width, None, axis=dim), axis, forward
        )
        high = lax.ppermute(lax.slice_in_dim(block, 0, width, axis=dim), axis, backward)
        block = jnp.concatenate([low, block, high], axis=dim)
    return block


def prefix(value, axis, combine, identity):
    size, position = (lax.axis_size(axis), lax.axis_index(axis))
    everything = lax.all_gather(value.astype(jnp.bfloat16), axis)
    start = jnp.broadcast_to(jnp.asarray(identity, value.dtype), value.shape)

    def lap(k, before):
        reached = k < position
        new = combine(before, everything[k].astype(value.dtype))
        return jnp.where(reached, new, before)

    return lax.fori_loop(0, size, lap, start)


def time_mod(times, mod_weight):
    half = mod_weight.shape[0] // 2
    freqs = jnp.exp(-math.log(10000.0) * jnp.arange(half, dtype=jnp.float32) / half)
    angle = 1000.0 * times[:, None] * freqs[None, :]
    embed = jnp.concatenate([jnp.cos(angle), jnp.sin(angle)], axis=1)
    act = jax.nn.silu(embed).astype(jnp.bfloat16)
    return jnp.dot(act, mod_weight, preferred_element_type=jnp.float32)


def modulate(state, shift, scale):
    values = state.astype(jnp.float32)
    center = values - jnp.mean(values, -1, keepdims=True)
    spread = jnp.mean(center * center, -1, keepdims=True)
    return (center / jnp.sqrt(spread + 1e-06) * (1.0 + scale) + shift).astype(jnp.bfloat16)


def head_norm(values):
    return (values / jnp.sqrt(jnp.mean(values * values, -1, keepdims=True) + 1e-06)).astype(
        jnp.bfloat16
    )


def body(start, trajectory, plan, neighbors, mod_weight, w_qkv, w_out):
    steps_here, tok_here, width = trajectory.shape
    tile = tok_here // 2
    rows = steps_here * tok_here
    times = plan.astype(jnp.float32) / NSCHED
    first = lax.axis_index("tm") * steps_here
    own_times = lax.dynamic_slice_in_dim(times, first, steps_here + 1)
    steps = own_times[:-1] - own_times[1:]
    mod = time_mod(own_times[:steps_here], mod_weight)
    normed = modulate(trajectory, mod[:, None, :width], mod[:, None, width:])
    flat = normed.reshape(rows, width)
    columns = flat
    qkv = jnp.dot(
        columns,
        lax.all_gather(w_qkv, "tok", axis=0, tiled=True),
        preferred_element_type=jnp.float32,
    )
    query = head_norm(qkv[:, :width].reshape(steps_here, 2, tile, HEADS, HEAD_DIM))
    keys_own = head_norm(qkv[:, width : 2 * width].reshape(rows, HEADS, HEAD_DIM)).reshape(
        steps_here, tok_here, width
    )
    values_own = qkv[:, 2 * width :].astype(jnp.bfloat16).reshape(steps_here, tok_here, width)
    stacked = jnp.stack([keys_own, values_own])
    wide_kv = padded(stacked, (("tok", 2),), tok_here)
    kv_tiles = wide_kv.reshape(2, steps_here, 6, tile, width)
    local = neighbors - (2 * lax.axis_index("tok") - 2)
    onehot = (local[:, :, None] == jnp.arange(6, dtype=jnp.int32)[None, None, :]).astype(
        jnp.bfloat16
    )
    picked = jnp.einsum("cnl,pslrd->pscnrd", onehot, kv_tiles, preferred_element_type=jnp.float32)
    picked = picked.astype(jnp.bfloat16).reshape(2, steps_here, 2, NB * tile, HEADS, HEAD_DIM)
    score = jnp.einsum(
        "sctha,sckha->schtk", query, picked[0], preferred_element_type=jnp.float32
    ) / math.sqrt(HEAD_DIM)
    expo = jnp.exp(score)
    prob = (expo / jnp.sum(expo, -1, keepdims=True)).astype(jnp.bfloat16)
    attn = jnp.einsum("schtk,sckha->sctha", prob, picked[1], preferred_element_type=jnp.float32)
    attn = attn.astype(jnp.bfloat16).reshape(rows, width)
    columns = attn
    drift = jnp.dot(
        columns,
        lax.all_gather(w_out, "tok", axis=0, tiled=True),
        preferred_element_type=jnp.float32,
    )
    scaled = steps[:, None, None] * drift.reshape(steps_here, tok_here, width)
    before_local = jnp.cumsum(scaled, axis=0) - scaled
    device_total = jnp.sum(scaled, axis=0)
    earlier = prefix(
        device_total,
        "tm",
        lambda first_sum, later_sum: first_sum + later_sum,
        jnp.zeros_like(device_total),
    )
    return start.astype(jnp.float32)[None] - (earlier[None] + before_local)


def solution(mesh):
    return jax.shard_map(
        body,
        mesh=mesh,
        in_specs=(
            P("tok", None),
            P("tm", "tok", None),
            P(),
            P("tok", None),
            P(),
            P("tok", None),
            P("tok", None),
        ),
        out_specs=P("tm", "tok", None),
        check_vma=False,
    )
```

profile of v0, /device:TPU:32, one launch (start us, length us, event | category | flops | bytes accessed | tf_op | source)
XLA Modules:
  0.0 314.9 jit_solution(16251401336110675667)
XLA Ops:
  10.3 125.9 %all-gather.5.cloned.1.call-done = bf16[1536,4608]{1,0:T(8,128)(2,1)} async-done(((bf16[48,4608]{1,0:T(8,128)(2,1)}), bf16[1536,4608]{1,0:T(8,128)(2,1)}) %all-gather.5.cloned.1.call-update) | async-done | bytes 14155792 | tf_op jit(solution)/shard_map/all_gather | solution.py:76
  136.2 7.0 %fusion.41 = f32[256,4608]{1,0:T(8,128)S(1)} fusion(bf16[256,1536]{1,0:T(8,128)(2,1)S(1)} %bitcast.45, bf16[1536,4608]{1,0:T(8,128)(2,1)} %all-gather.5.cloned.1.call-done), kind=kOutput, calls=%fused_computation.62 | convolution fusion | flops 3623878656 | bytes 19660800 | tf_op jit(solution)/shard_map/dot_general | solution.py:74
  144.2 2.2 fusion.39
  148.0 3.7 %copy.10 = f32[1,2,128,1536]{2,1,3,0:T(2,128)} copy(f32[1,2,128,1536]{3,2,1,0:T(8,128)} %bitcast.42) | data formatting | bytes 3145728 | tf_op jit(solution)/shard_map/reshape | solution.py:80
  152.4 2.0 divide_convert_fusion.3
  154.4 3.2 %pad_maximum_fusion.1 = bf16[2,2,128,1536]{2,1,3,0:T(2,128)(2,1)} fusion(bf16[1,2,128,1536]{2,1,3,0:T(2,128)(2,1)S(1)} %copy.11, bf16[1,2,128,1536]{2,1,3,0:T(2,128)(2,1)S(1)} %divide_convert_fusion.3), kind=kLoop, calls=%fused_computation.29 | loop fusion | flops 786432 | bytes 3145728 | tf_op jit(solution)/shard_map/stack | solution.py:84
  157.6 2.2 collective-permute-start
  159.8 3.6 %collective-permute-start.1 = (bf16[2,2,128,1536]{2,1,3,0:T(2,128)(2,1)}, bf16[2,2,128,1536]{2,1,3,0:T(2,128)(2,1)}, u32[]{:S(2)}, u32[]{:S(2)}) collective-permute-start(bf16[2,2,128,1536]{2,1,3,0:T(2,128)(2,1)} %pad_maximum_fusion.1), channel_id=1, source_target_pairs={{1,0},{2,1},{3,2},{4,3},{5,4},{6,5},{7,6},{8,7},{9,8},{10,9},{11,1... | collective-permute-start | bytes 4718600 | tf_op jit(solution)/shard_map/ppermute | solution.py:22
  163.4 1.6 reshape.100
  165.0 2.4 multiply_reduce_fusion
  167.5 1.5 divide_convert_fusion.1
  169.0 13.6 %collective-permute-done = bf16[2,2,128,1536]{2,1,3,0:T(2,128)(2,1)} collective-permute-done((bf16[2,2,128,1536]{2,1,3,0:T(2,128)(2,1)}, bf16[2,2,128,1536]{2,1,3,0:T(2,128)(2,1)}, u32[]{:S(2)}, u32[]{:S(2)}) %collective-permute-start) | collective-permute-done | bytes 1572896 | tf_op jit(solution)/shard_map/ppermute | solution.py:19
  183.5 7.7 %pad_maximum_fusion = bf16[2,2,384,1536]{2,1,3,0:T(2,128)(2,1)} fusion(bf16[2,2,128,1536]{2,1,3,0:T(2,128)(2,1)} %collective-permute-done.1, bf16[1,2,128,1536]{2,1,3,0:T(2,128)(2,1)S(1)} %copy.11, bf16[1,2,128,1536]{2,1,3,0:T(2,128)(2,1)S(1)} %divide_convert_fusion.3, bf16[2,2,128,1536]{2,1,3,0:T(2,128)(2,1)} %collective-permute-done), kind=kLoop, calls=%fused_computation.4 | loop fusion | flops 18874368 | bytes 9437184 | tf_op jit(solution)/shard_map/concatenate | solution.py:23
  191.3 12.4 %copy.12 = bf16[2,2,384,1536]{3,2,1,0:T(8,128)(2,1)} copy(bf16[2,2,384,1536]{2,1,3,0:T(2,128)(2,1)} %pad_maximum_fusion) | data formatting | bytes 9437184 | tf_op jit(solution)/shard_map/concatenate | solution.py:23
  203.7 9.1 %fusion = bf16[2,2,2,3,64,1536]{5,3,2,4,1,0:T(4,128)(2,1)S(1)} fusion(bf16[2,2,6,64,1536,1]{4,3,2,1,0,5:T(8,128)(2,1)} %bitcast.40, s32[2,3]{1,0:T(2,128)S(1)} %broadcast_subtract_fusion), kind=kOutput, calls=%fused_computation.2 | convolution fusion | flops 30670884 | bytes 9437208 | tf_op jit(solution)/shard_map/cnl,pslrd->pscnrd/dot_general | solution.py:91
  212.8 3.6 %fusion.38 = (bf16[1,2,2,3,64,1536]{5,3,2,4,1,0:T(4,128)(2,1)S(1)}, bf16[1,2,2,3,64,1536]{5,3,2,4,1,0:T(4,128)(2,1)}) fusion(bf16[2,2,2,3,64,1536]{5,3,2,4,1,0:T(4,128)(2,1)S(1)} %fusion), kind=kLoop, calls=%fused_computation.59 | loop fusion | bytes 9437184 | tf_op jit(solution)/shard_map/slice | solution.py:94
  216.4 2.3 copy.15
  218.7 5.4 %squeeze.12 = bf16[2,2,192,12,128]{4,3,2,1,0:T(8,128)(2,1)} reshape(bf16[1,2,2,3,64,1536]{5,4,3,2,1,0:T(8,128)(2,1)} %copy.15) | data formatting | bytes 4718592 | tf_op jit(solution)/shard_map/squeeze | solution.py:94
  224.2 4.2 %copy.14 = bf16[1,2,2,3,64,1536]{5,4,3,2,1,0:T(8,128)(2,1)} copy(bf16[1,2,2,3,64,1536]{5,3,2,4,1,0:T(4,128)(2,1)} %get-tuple-element.109) | data formatting | bytes 4718592 | tf_op jit(solution)/shard_map/slice | solution.py:98
  228.4 5.5 %squeeze.11 = bf16[2,2,192,12,128]{4,3,2,1,0:T(8,128)(2,1)} reshape(bf16[1,2,2,3,64,1536]{5,4,3,2,1,0:T(8,128)(2,1)} %copy.14) | data formatting | bytes 4718592 | tf_op jit(solution)/shard_map/squeeze | solution.py:98
  234.0 3.8 %fusion.8 = (f32[2,2,12,64]{3,2,1,0:T(8,128)S(1)}, f32[2,2,12,64,192]{4,3,2,1,0:T(8,128)S(1)}) fusion(bf16[2,2,192,12,128]{4,3,2,1,0:T(8,128)(2,1)} %squeeze.12, bf16[2,2,64,12,128]{4,3,2,1,0:T(8,128)(2,1)S(1)} %copy-done.5), kind=kOutput, calls=%fused_computation.12 | convolution fusion | flops 152171520 | bytes 5517312 | tf_op jit(solution)/shard_map/sctha,sckha->schtk/dot_general | solution.py:93
  237.7 1.5 fusion.24
  240.4 5.8 %fusion.40 = (bf16[128,1536]{1,0:T(8,128)(2,1)}, f32[2,128,1536]{2,1,0:T(8,128)}) fusion(bf16[2,128,1536]{2,1,0:T(8,128)(2,1)S(1)} %dot_general.25, bf16[1536,1536]{1,0:T(8,128)(2,1)} %all-gather.7.cloned.1.call-done, f32[2]{0:T(128)S(1)} %get-tuple-element.117), kind=kOutput, calls=%fused_computation.61 | convolution fusion | flops 1208549376 | bytes 7471112 | tf_op jit(solution)/shard_map/dot_general | solution.py:101
  246.2 47.2 %all-gather.9.cloned.1.call-done = bf16[1024,1536]{1,0:T(8,128)(2,1)} async-done(((bf16[128,1536]{1,0:T(8,128)(2,1)}), bf16[1024,1536]{1,0:T(8,128)(2,1)}) %all-gather.9.cloned.1.call-update) | async-done | bytes 3145744 | tf_op jit(solution)/shard_map/all_gather | solution.py:29
  293.4 11.5 %while.14 = (s32[]{:T(128)}, f32[128,1536]{1,0:T(8,128)S(1)}, s32[]{:T(128)}, bf16[8,128,1536]{2,1,0:T(8,128)(2,1)}, s32[]{:T(128)}, /*index=5*/s32[]{:T(128)}) while((s32[]{:T(128)}, f32[128,1536]{1,0:T(8,128)S(1)}, s32[]{:T(128)}, bf16[8,128,1536]{2,1,0:T(8,128)(2,1)}, s32[]{:T(128)}, /*index=5*/s32[]{:T(128)}) %tuple.49), condition=%wide.region_7.8_spmd.clone, body=%wide.region_6.7_spmd.clone.sunk | while | flops 786436 | bytes 1966173 | solution.py:37
  294.9 1.4 add_select_fusion.2
  296.3 1.4 add_select_fusion.2
  299.2 1.4 add_select_fusion.2
  300.7 1.4 add_select_fusion.2
  302.1 1.4 add_select_fusion.2
  303.5 1.4 add_select_fusion.2
  305.0 3.4 %fusion.9 = f32[2,128,1536]{2,1,0:T(8,128)} fusion(f32[2,128,1536]{2,1,0:T(8,128)} %get-tuple-element.122, f32[128,1536]{1,0:T(8,128)S(1)} %get-tuple-element.84, f32[128,1536]{1,0:T(8,128)S(1)} %convert_element_type.68), kind=kOutput, calls=%fused_computation.13 | output fusion | flops 1572864 | bytes 4718592 | tf_op jit(solution)/shard_map/jit(cumsum)/reduce_window_sum | solution.py:107
  (55 shorter events, 11.8 us)
Async XLA Ops:
  6.5 2.5 copy-start
  6.5 2.8 copy-start.3
  6.5 129.7 %all-gather.5.cloned.1.call-start = ((), (), s32[]{:S(2)}) async-start(), calls=%async_computation | async-start | bytes 14598144 | tf_op jit(solution)/shard_map/all_gather | solution.py:76
  7.3 233.1 %all-gather.7.cloned.1.call-start = ((), (), s32[]{:S(2)}) async-start(), calls=%async_computation.1 | async-start | bytes 4866048 | tf_op jit(solution)/shard_map/all_gather | solution.py:103
  8.0 285.4 %all-gather.9.cloned.1.call-start = ((), (), s32[]{:S(2)}) async-start(), calls=%async_computation.2 | async-start | bytes 3538944 | tf_op jit(solution)/shard_map/all_gather | solution.py:29
  148.0 3.8 %copy-start.6 = (bf16[256,1536]{1,0:T(8,128)(2,1)S(1)}, bf16[256,1536]{1,0:T(8,128)(2,1)}, u32[]{:S(2)}) copy-start(bf16[256,1536]{1,0:T(8,128)(2,1)} %slice.53) | copy-start | bytes 2359300
  154.4 9.0 %copy-start.9 = (s32[2,3]{1,0:T(2,128)S(1)}, s32[2,3]{1,0:T(2,128)}, u32[]{:S(2)}) copy-start(s32[2,3]{1,0:T(2,128)} %param.12) | copy-start | bytes 76
  154.4 9.0 %copy-start.4 = (f32[256,1536]{1,0:T(8,128)S(1)}, f32[256,1536]{1,0:T(8,128)}, u32[]{:S(2)}) copy-start(f32[256,1536]{1,0:T(8,128)} %get-tuple-element.110) | copy-start | bytes 4718596
  157.6 25.0 %collective-permute-start = (bf16[2,2,128,1536]{2,1,3,0:T(2,128)(2,1)}, bf16[2,2,128,1536]{2,1,3,0:T(2,128)(2,1)}, u32[]{:S(2)}, u32[]{:S(2)}) collective-permute-start(bf16[2,2,128,1536]{2,1,3,0:T(2,128)(2,1)} %pad_maximum_fusion.1), channel_id=1, source_target_pairs={{0,1},{1,2},{2,3},{3,4},{4,5},{5,6},{6,7},{7,8},{8,9},{9,10},{10,1... | collective-permute-start | bytes 4718600 | tf_op jit(solution)/shard_map/ppermute | solution.py:19
  159.8 23.7 %collective-permute-start.1 = (bf16[2,2,128,1536]{2,1,3,0:T(2,128)(2,1)}, bf16[2,2,128,1536]{2,1,3,0:T(2,128)(2,1)}, u32[]{:S(2)}, u32[]{:S(2)}) collective-permute-start(bf16[2,2,128,1536]{2,1,3,0:T(2,128)(2,1)} %pad_maximum_fusion.1), channel_id=1, source_target_pairs={{1,0},{2,1},{3,2},{4,3},{5,4},{6,5},{7,6},{8,7},{9,8},{10,9},{11,1... | collective-permute-start | bytes 4718600 | tf_op jit(solution)/shard_map/ppermute | solution.py:22
  165.0 2.4 copy-start.2
  228.4 5.5 %copy-start.5 = (bf16[2,2,64,12,128]{4,3,2,1,0:T(8,128)(2,1)S(1)}, bf16[2,2,64,12,128]{4,3,2,1,0:T(8,128)(2,1)}, u32[]{:S(2)}) copy-start(bf16[2,2,64,12,128]{4,3,2,1,0:T(8,128)(2,1)} %divide_convert_fusion.1) | copy-start | bytes 2359300
  234.0 3.8 %copy-start.7 = (bf16[2,2,192,12,128]{4,3,2,1,0:T(8,128)(2,1)S(1)}, bf16[2,2,192,12,128]{4,3,2,1,0:T(8,128)(2,1)}, u32[]{:S(2)}) copy-start(bf16[2,2,192,12,128]{4,3,2,1,0:T(8,128)(2,1)} %squeeze.11) | copy-start | bytes 7077892
  240.3 5.8 %copy-start.8 = (bf16[128,1536]{1,0:T(8,128)(2,1)S(1)}, bf16[128,1536]{1,0:T(8,128)(2,1)}, u32[]{:S(2)}) copy-start(bf16[128,1536]{1,0:T(8,128)(2,1)} %param.9) | copy-start | bytes 1179652
  305.0 3.4 %copy-start.1 = (bf16[256,3072]{1,0:T(8,128)(2,1)S(1)}, bf16[256,3072]{1,0:T(8,128)(2,1)}, u32[]{:S(2)}) copy-start(bf16[256,3072]{1,0:T(8,128)(2,1)} %param.13) | copy-start | bytes 4718596
Sparse Core Ops, SparseCore 0:
  10.1 126.0 all-gather.4
  139.0 85.8 all-gather.6
  246.3 47.1 all-gather.8
where the time goes:
time: 316 us; the launch traced here: 315 us
  waiting for transfers between devices  189 us (60%)
  local copies, waits for them, and re-layouts  43.1 us (14%)
  other arithmetic  35.8 us (11%)
  matrix products  27.5 us (9%)
  between operations  13.4 us (4%)
  starting transfers between devices  5.81 us (2%)
    all_gather x1, waiting for transfers between devices, body(): lax.all_gather(w_qkv, 'tok', axis=0, tiled=True)  126 us
    all_gather x1, waiting for transfers between devices, prefix(): everything = lax.all_gather(value.astype(jnp.bfloat16), axis)  47.2 us
    ppermute x1, waiting for transfers between devices, padded(): lax.ppermute(lax.slice_in_dim(block, block.shape[dim] - width, None, axis...  13.6 us
    concatenate x1, local copies, waits for them, and re-layouts, padded(): block = jnp.concatenate([low, block, high], axis=dim)  12.4 us
    select_n x8, other arithmetic, lap(): return jnp.where(reached, new, before)  11.4 us
    dot_general x1, matrix products, body(): jnp.einsum('cnl,pslrd->pscnrd', onehot, kv_tiles, preferred_element_type=...  9.1 us
    concatenate x1, other arithmetic, padded(): block = jnp.concatenate([low, block, high], axis=dim)  7.74 us
    dot_general x1, matrix products, body(): jnp.dot(columns, lax.all_gather(w_qkv, 'tok', axis=0, tiled=True), prefer...  7.03 us
  transfers between devices with their start and end apart: 5, of which 4 were waited for; matrix products, arithmetic and copies ran while one was open for 27% of the time, Pallas kernels for 0%

commit v1 on v0

v1 whole, which is shorter than its diff:
```python
import functools
import math

import jax
import jax.numpy as jnp
from jax import lax
from jax.experimental import pallas as pl
from jax.experimental.pallas import tpu as pltpu
from jax.sharding import PartitionSpec as P

NSCHED = 1000
XG = 4
ZG = 8
HL = 3
HD = 128
CW = HL * HD
TILE = 64
MESH = pl.DeviceIdType.MESH


def time_mod(times, mod_weight):
    half = mod_weight.shape[0] // 2
    freqs = jnp.exp(-math.log(10000.0) * jnp.arange(half, dtype=jnp.float32) / half)
    angle = 1000.0 * times[:, None] * freqs[None, :]
    embed = jnp.concatenate([jnp.cos(angle), jnp.sin(angle)], axis=1)
    act = jax.nn.silu(embed).astype(jnp.bfloat16)
    return jnp.dot(act, mod_weight, preferred_element_type=jnp.float32)


def modulate(state, shift, scale):
    values = state.astype(jnp.float32)
    center = values - jnp.mean(values, -1, keepdims=True)
    spread = jnp.mean(center * center, -1, keepdims=True)
    return (center / jnp.sqrt(spread + 1e-06) * (1.0 + scale) + shift).astype(jnp.bfloat16)


class Ring:
    def __init__(self, buf, send, recv, pos, peers):
        self.buf, self.send, self.recv = buf, send, recv
        self.yh, self.z, self.c = pos
        self.peers = peers
        self.sent = []

    def block(self, yh, z):
        return self.buf.at[yh, z, self.c]

    def push(self, ref, i, peer):
        copy = pltpu.make_async_remote_copy(
            src_ref=ref, dst_ref=ref, send_sem=self.send.at[i], recv_sem=self.recv.at[i],
            device_id=self.peers[peer], device_id_type=MESH,
        )
        copy.start()
        self.sent.append(copy)

    def arrive(self, ref, i, peer):
        pltpu.make_async_remote_copy(
            src_ref=ref, dst_ref=ref, send_sem=self.send.at[i], recv_sem=self.recv.at[i],
            device_id=self.peers[peer], device_id_type=MESH,
        ).wait_recv()

    def own(self):
        mine = self.block(self.yh, self.z)
        self.push(mine, 0, "z+")
        self.push(mine, 4, "z-")
        self.push(mine, 7, "part")

    def step(self, s):
        low = self.block(self.yh, lax.rem(self.z + ZG - s, ZG))
        self.arrive(low, s - 1, "z+")
        if s < 4:
            self.push(low, s, "z+")
        self.push(low, 7 + s, "part")
        if s < 4:
            high = self.block(self.yh, lax.rem(self.z + s, ZG))
            self.arrive(high, 3 + s, "z-")
            if s < 3:
                self.push(high, 4 + s, "z-")
            self.push(high, 11 + s, "part")

    def share_own(self):
        self.push(self.buf.at[self.yh, :, self.c], 15, "core")

    def share_other(self):
        other = 1 - self.yh
        self.arrive(self.block(other, self.z), 7, "part")
        for s in range(1, 5):
            self.arrive(self.block(other, lax.rem(self.z + ZG - s, ZG)), 7 + s, "part")
            if s < 4:
                self.arrive(self.block(other, lax.rem(self.z + s, ZG)), 11 + s, "part")
        self.push(self.buf.at[other, :, self.c], 16, "core")

    def shared(self):
        self.arrive(self.buf.at[self.yh, :, 1 - self.c], 15, "core")
        self.arrive(self.buf.at[1 - self.yh, :, 1 - self.c], 16, "core")

    def finish(self):
        for copy in self.sent:
            copy.wait_send()


def kernel(
    h_ref, wqkv_ref, wout_ref, start_ref, nb_ref, step_ref, out_ref,
    hbuf, wbuf, wo, kv0, kv1, kv2, kv3, abuf, tsend, trecv, sbuf, sall,
    lsem, hs, hr, ws, wr, os, orecv, ks, kr, ts, tr, ss, sr,
):
    tm, tok = lax.axis_index("tm"), lax.axis_index("tok")
    x, yl = lax.rem(tm, XG), lax.div(tm, XG)
    yh, z, c = lax.div(tok, 2 * ZG), lax.div(lax.rem(tok, 2 * ZG), 2), lax.rem(tok, 2)
    width = h_ref.shape[1]
    rows = h_ref.shape[0]
    part_rows = rows // 2
    ntok = 4 * ZG

    def at_x(k):
        return {"tm": yl * XG + lax.rem(x + k, XG), "tok": tok}

    def at_tok(k):
        return {"tm": tm, "tok": lax.rem(tok + ntok + k, ntok)}

    peers = {
        "z+": {"tm": tm, "tok": yh * 2 * ZG + lax.rem(z + 1, ZG) * 2 + c},
        "z-": {"tm": tm, "tok": yh * 2 * ZG + lax.rem(z + ZG - 1, ZG) * 2 + c},
        "core": {"tm": tm, "tok": yh * 2 * ZG + z * 2 + 1 - c},
        "part": {"tm": (1 - yl) * XG + x, "tok": (1 - yh) * 2 * ZG + z * 2 + c},
    }
    lower = {"tm": (1 - yl) * XG + x, "tok": tok}
    beside = at_tok(2 * c - 1)

    barrier = pltpu.get_barrier_semaphore()
    everyone = [at_x(1), at_x(2), at_x(3), *peers.values(), lower, beside]
    for peer in everyone:
        pl.semaphore_signal(barrier, inc=1, device_id=peer, device_id_type=MESH)
    pl.semaphore_wait(barrier, len(everyone))

    sent = []

    def remote(src, dst, s, r, i, peer):
        return pltpu.make_async_remote_copy(
            src_ref=src, dst_ref=dst, send_sem=s.at[i], recv_sem=r.at[i],
            device_id=peer, device_id_type=MESH,
        )

    def push(*args):
        copy = remote(*args)
        copy.start()
        sent.append(copy)

    top, bottom = pl.ds(0, part_rows), pl.ds(part_rows, part_rows)

    own_copies = []
    for j in range(3):
        column = pl.multiple_of(j * width + x * CW, HD)
        own_copies.append(pltpu.make_async_copy(
            wqkv_ref.at[:, pl.ds(column, CW)],
            wbuf.at[yh, z, c, :, pl.ds(j * CW, CW)], lsem.at[j],
        ))
    own_copies.append(pltpu.make_async_copy(wout_ref, wo.at[yh, z, c], lsem.at[3]))
    for copy in own_copies:
        copy.start()

    push(h_ref.at[top], hbuf.at[0, top], hs, hr, 0, at_x(1))
    push(h_ref.at[bottom], hbuf.at[0, bottom], hs, hr, 1, at_x(3))
    for copy in own_copies:
        copy.wait()
    pos = (yh, z, c)
    wring = Ring(wbuf, ws, wr, pos, peers)
    oring = Ring(wo, os, orecv, pos, peers)
    wring.own()
    push(h_ref.at[bottom], hbuf.at[1, top], hs, hr, 2, at_x(1))
    push(h_ref.at[top], hbuf.at[1, bottom], hs, hr, 3, at_x(3))

    def h_arrive(group):
        i = 2 * group
        remote(hbuf.at[group, top], hbuf.at[group, top], hs, hr, i, at_x(1)).wait_recv()
        remote(hbuf.at[group, bottom], hbuf.at[group, bottom], hs, hr, i + 1, at_x(3)).wait_recv()

    wring.step(1)
    wring.step(2)
    wring.step(3)
    h_arrive(0)
    push(hbuf.at[0, top], hbuf.at[2, top], hs, hr, 4, at_x(1))
    push(hbuf.at[0, bottom], hbuf.at[2, bottom], hs, hr, 5, at_x(3))
    wring.step(4)
    wring.share_own()
    oring.own()
    oring.step(1)
    oring.step(2)
    wring.share_other()
    wring.shared()

    kvs = (kv0, kv1, kv2, kv3)

    def qkv(group):
        kv = kvs[group]

        def one(j, carry):
            column = pl.multiple_of(j * CW, HD)
            left = h_ref[...] if group == 0 else hbuf[group - 1]
            right = wbuf[:, :, :, :, pl.ds(column, CW)].reshape(width, CW)
            part = jnp.dot(left, right, preferred_element_type=jnp.float32)
            pieces = []
            for head in range(HL):
                piece = part[:, head * HD : (head + 1) * HD]
                norm = lax.rsqrt(jnp.mean(piece * piece, -1, keepdims=True) + 1e-06)
                pieces.append(piece * jnp.where(j < 2, norm, 1.0))
            done = jnp.concatenate(pieces, axis=1).astype(jnp.bfloat16)
            for half in range(2):
                for tile in range(2):
                    first = half * part_rows + tile * TILE
                    kv[2 + tile, j, half] = done[first : first + TILE]
            return carry

        lax.fori_loop(0, 3, one, 0)
        push(kv.at[2:4, 1:3], kv.at[0:2, 1:3], ks, kr, 2 * group, at_tok(1))
        push(kv.at[2:4, 1:3], kv.at[4:6, 1:3], ks, kr, 2 * group + 1, at_tok(-1))

    def attend(group):
        kv = kvs[group]
        remote(kv.at[0:2, 1:3], kv.at[0:2, 1:3], ks, kr, 2 * group, at_tok(1)).wait_recv()
        remote(kv.at[4:6, 1:3], kv.at[4:6, 1:3], ks, kr, 2 * group + 1, at_tok(-1)).wait_recv()

        def one(i, carry):
            half, tile = lax.div(i, 2), lax.rem(i, 2)
            if group == 0:
                when = 2 * x + half
            elif group == 3:
                when = 2 * lax.rem(x + 2, XG) + half
            elif group == 1:
                when = 2 * lax.rem(x + 3 + 2 * half, XG) + half
            else:
                when = 2 * lax.rem(x + 3 + 2 * half, XG) + 1 - half
            step = step_ref[0, when]
            near = [
                jnp.clip(nb_ref[tile, n] - (2 * tok - 2), 0, 5) for n in range(nb_ref.shape[1])
            ]
            query = kv[2 + tile, 0, half]
            keys = jnp.concatenate([kv[n, 1, half] for n in near], axis=0)
            values = jnp.concatenate([kv[n, 2, half] for n in near], axis=0)
            outs = []
            for head in range(HL):
                cols = slice(head * HD, (head + 1) * HD)
                score = lax.dot_general(
                    query[:, cols], keys[:, cols], (((1,), (1,)), ((), ())),
                    preferred_element_type=jnp.float32,
                ) * (1.0 / math.sqrt(HD))
                expo = jnp.exp(score)
                total = jnp.sum(expo, -1, keepdims=True)
                mixed = jnp.dot(
                    expo.astype(jnp.bfloat16), values[:, cols], preferred_element_type=jnp.float32
                )
                outs.append(mixed * (step / total))
            abuf[when, pl.ds(pl.multiple_of(tile * TILE, TILE), TILE), :] = jnp.concatenate(
                outs, axis=1
            )
            return carry

        lax.fori_loop(0, 4, one, 0)

    qkv(0)
    oring.step(3)
    qkv(1)
    oring.step(4)
    oring.share_own()
    attend(0)
    h_arrive(1)
    qkv(2)
    attend(1)
    h_arrive(2)
    qkv(3)
    attend(2)
    attend(3)

    total = abuf[0]
    for k in range(1, 2 * XG):
        total = total + abuf[k]
    tsend[...] = total.astype(jnp.bfloat16)
    push(tsend, trecv, ts, tr, 0, lower)
    remote(trecv, trecv, ts, tr, 0, lower).wait_recv()
    run = jnp.where(yl > 0, trecv[...].astype(jnp.float32), 0.0)
    for k in range(2 * XG):
        sbuf[k] = run.astype(jnp.bfloat16)
        if k < 2 * XG - 1:
            run = run + abuf[k]

    def columns_of(src):
        return sall.at[:, :, pl.ds(pl.multiple_of(src * CW, HD), CW)]

    for k in range(1, XG):
        push(sbuf.at[pl.ds(2 * lax.rem(x + k, XG), 2)], columns_of(x), ss, sr, k - 1, at_x(k))
    keep = pltpu.make_async_copy(sbuf.at[pl.ds(2 * x, 2)], columns_of(x), lsem.at[4])
    keep.start()
    oring.share_other()
    oring.shared()
    keep.wait()
    for k in range(1, XG):
        source = columns_of(lax.rem(x + XG - k, XG))
        remote(source, source, ss, sr, k - 1, at_x(k)).wait_recv()

    chunk = 256

    def finish(i, carry):
        column = pl.ds(pl.multiple_of(i * chunk, chunk), chunk)
        left = sall[...].reshape(rows, width)
        right = wo[:, :, :, :, column].reshape(width, chunk)
        before = jnp.dot(left, right, preferred_element_type=jnp.float32)
        first = start_ref[:, column].astype(jnp.float32)
        out_ref[0, :, column] = first - before[:part_rows]
        out_ref[1, :, column] = first - before[part_rows:]
        return carry

    lax.fori_loop(0, width // chunk, finish, 0)
    wring.finish()
    oring.finish()
    for copy in sent:
        copy.wait_send()


def body(start, trajectory, plan, neighbors, mod_weight, w_qkv, w_out):
    steps_here, tok_here, width = trajectory.shape
    rows = steps_here * tok_here
    times = plan.astype(jnp.float32) / NSCHED
    steps = times[:-1] - times[1:]
    tm = lax.axis_index("tm")
    own_times = lax.dynamic_slice_in_dim(times, tm * steps_here, steps_here)
    ring_steps = lax.dynamic_slice_in_dim(
        steps, lax.div(tm, XG) * XG * steps_here, XG * steps_here
    )[None]
    mod = time_mod(own_times, mod_weight)
    h = modulate(trajectory, mod[:, None, :width], mod[:, None, width:]).reshape(rows, width)
    bf, f32 = jnp.bfloat16, jnp.float32
    kv = pltpu.VMEM((6, 3, steps_here, TILE, CW), bf)
    dma = pltpu.SemaphoreType.DMA
    vmem = pl.BlockSpec(memory_space=pltpu.VMEM)
    smem = pl.BlockSpec(memory_space=pltpu.SMEM)
    hbm = pl.BlockSpec(memory_space=pl.ANY)
    return pl.pallas_call(
        kernel,
        out_shape=jax.ShapeDtypeStruct((steps_here, tok_here, width), f32),
        in_specs=[vmem, hbm, hbm, vmem, smem, smem],
        out_specs=vmem,
        scratch_shapes=[
            pltpu.VMEM((3, rows, width), bf),
            pltpu.VMEM((2, ZG, 2, w_qkv.shape[0], 3 * CW), bf),
            pltpu.VMEM((2, ZG, 2, w_out.shape[0], width), bf),
            kv, kv, kv, kv,
            pltpu.VMEM((2 * XG, tok_here, CW), f32),
            pltpu.VMEM((tok_here, CW), bf),
            pltpu.VMEM((tok_here, CW), bf),
            pltpu.VMEM((2 * XG, tok_here, CW), bf),
            pltpu.VMEM((steps_here, tok_here, width), bf),
            dma((5,)),
            dma((6,)), dma((6,)),
            dma((17,)), dma((17,)),
            dma((17,)), dma((17,)),
            dma((8,)), dma((8,)),
            dma((1,)), dma((1,)),
            dma((3,)), dma((3,)),
        ],
        compiler_params=pltpu.CompilerParams(collective_id=0, has_side_effects=True),
    )(h, w_qkv, w_out, start, neighbors, ring_steps)


def solution(mesh):
    return jax.shard_map(
        body,
        mesh=mesh,
        in_specs=(
            P("tok", None),
            P("tm", "tok", None),
            P(),
            P("tok", None),
            P(),
            P("tok", None),
            P("tok", None),
        ),
        out_specs=P("tm", "tok", None),
        check_vma=False,
    )
```

time: 316 us -> 98.5 us (0.31)
  waiting for transfers between devices: 189 us -> 0 us
  Pallas kernels: 0 us -> 89.4 us
  local copies, waits for them, and re-layouts: 43.1 us -> 3.28 us
  other arithmetic: 35.8 us -> 5.2 us
  matrix products: 27.5 us -> 0.32 us
  between operations: 13.4 us -> 0.05 us
  starting transfers between devices: 5.81 us -> 0 us
    all_gather x3 -> x0, waiting for transfers between devices: 173 us -> none  [the longest x1 126 us: body(): lax.all_gather(w_qkv, 'tok', axis=0, tiled=True)]
    pallas_call x0 -> x1, Pallas kernels: none -> 89.4 us  [body(): pl.pallas_call(kernel, out_shape=jax.ShapeDtypeStruct((steps_here, tok_he...]
    dot_general x5 -> x0, matrix products: 27.2 us -> none  [the longest x1 9.1 us: body(): jnp.einsum('cnl,pslrd->pscnrd', onehot, kv_tiles, preferred_element_type=...]
    ppermute x2 -> x0, waiting for transfers between devices: 14.6 us -> none  [the longest x1 13.6 us: padded(): lax.ppermute(lax.slice_in_dim(block, block.shape[dim] - width, None, axis...]
    concatenate x1 -> x0, local copies, waits for them, and re-layouts: 12.4 us -> none  [padded(): block = jnp.concatenate([low, block, high], axis=dim)]
    select_n x8 -> x0, other arithmetic: 11.4 us -> none  [lap(): return jnp.where(reached, new, before)]
    slice x4 -> x0, local copies, waits for them, and re-layouts: 11.1 us -> none  [the longest x2 5.94 us: body(): picked[0]]
    squeeze x2 -> x0, local copies, waits for them, and re-layouts: 11 us -> none  [the longest x1 5.53 us: body(): picked[1]]
  transfers between devices with their start and end apart: 5 -> 0, of which waited for: 4 -> 0; matrix products, arithmetic and copies ran while one was open for 27% -> 0% of each run, Pallas kernels for 0% -> 0%
where the time goes in v1:
time: 98.5 us; the launch traced here: 98.3 us
  Pallas kernels  89.4 us (91%)
  other arithmetic  5.2 us (5%)
  local copies, waits for them, and re-layouts  3.28 us (3%)
    pallas_call x1, Pallas kernels, body(): pl.pallas_call(kernel, out_shape=jax.ShapeDtypeStruct((steps_here, tok_he...  89.4 us
    unnamed x5, local copies, waits for them, and re-layouts  2.66 us

profile of v1, /device:TPU:32, one launch (start us, length us, event | category | flops | bytes accessed | tf_op | source)
XLA Modules:
  0.0 98.3 jit_solution(8654574144448377415)
XLA Ops:
  0.0 0.0 copy-start
  0.0 0.8 convert_multiply_fusion
  0.8 0.1 dynamic-slice_multiply_fusion
  0.9 0.1 slice_subtract_fusion
  0.9 0.6 dynamic-slice_bitcast_fusion.step_ref
  1.6 0.0 copy-start.1
  1.6 1.4 %convert_reduce_fusion = f32[2,128]{1,0:T(2,128)S(1)} fusion(bf16[2,128,1536]{2,1,0:T(8,128)(2,1)} %param.8), kind=kLoop, calls=%fused_computation.1 | loop fusion | flops 786176 | bytes 787456 | tf_op jit(solution)/shard_map/reduce_sum | solution.py:32
  3.0 1.5 %fusion.2 = f32[2,128]{1,0:T(2,128)S(1)} fusion(bf16[2,128,1536]{2,1,0:T(8,128)(2,1)} %param.8, f32[2,128]{1,0:T(2,128)S(1)} %broadcast_multiply_fusion), kind=kLoop, calls=%fused_computation.4 | loop fusion | flops 1572608 | bytes 788480 | tf_op jit(solution)/shard_map/reduce_sum | solution.py:33
  4.5 0.1 multiply_cosine_fusion
  4.6 0.0 copy-done
  4.6 0.3 fusion.7
  4.9 0.0 copy-done.1
  4.9 1.3 %fusion.5 = bf16[2,128,1536]{2,1,0:T(8,128)(2,1)} fusion(bf16[2,128,1536]{2,1,0:T(8,128)(2,1)S(1)} %copy-done.1, f32[2,1536]{1,0:T(2,128)S(1)} %get-tuple-element.6, f32[2,1536]{1,0:T(2,128)S(1)} %get-tuple-element.5, f32[2,128]{1,0:T(2,128)S(1)} %add_sqrt_fusion, f32[2,128]{1,0:T(2,128)S(1)} %broadcast_multiply_fusion), kind=kLoop, calls=%fused_computation.7 | loop fusion | flops 2359296 | bytes 1599488 | tf_op jit(solution)/shard_map/convert_element_type | solution.py:34
  6.2 89.4 %shard_map.73 = f32[2,128,1536]{2,1,0:T(8,128)} custom-call(bf16[256,1536]{1,0:T(8,128)(2,1)} %bitcast.4, bf16[48,4608]{1,0:T(8,128)(2,1)} %wqkv_ref.1, bf16[48,1536]{1,0:T(8,128)(2,1)} %wout_ref.1, bf16[128,1536]{1,0:T(8,128)(2,1)} %start_ref.1, s32[2,3]{1,0:T(2,128)} %nb_ref.1, f32[1,8]{1,0:T(1,128)} %dynamic-slice_bitcast_fusion.step_ref), custom_call_target="tpu_custom_call" | custom-call | tf_op jit(solution)/shard_map/pallas_call | solution.py:336
  95.6 2.7 %copy.9 = f32[2,128,1536]{2,1,0:T(8,128)} copy(f32[2,128,1536]{2,1,0:T(8,128)} %shard_map.73) | data formatting | bytes 3145728
  (4 shorter events, 0.0 us)
Async XLA Ops:
  0.0 4.6 %copy-start = (bf16[256,3072]{1,0:T(8,128)(2,1)S(1)}, bf16[256,3072]{1,0:T(8,128)(2,1)}, u32[]{:S(2)}) copy-start(bf16[256,3072]{1,0:T(8,128)(2,1)} %param.11) | copy-start | bytes 4718596
  1.6 3.4 %copy-start.1 = (bf16[2,128,1536]{2,1,0:T(8,128)(2,1)S(1)}, bf16[2,128,1536]{2,1,0:T(8,128)(2,1)}, u32[]{:S(2)}) copy-start(bf16[2,128,1536]{2,1,0:T(8,128)(2,1)} %param.8) | copy-start | bytes 2359300

commit v2 on v1

--- a/solution.py
+++ b/solution.py
@@ -35,67 +35,115 @@
 
 
 class Ring:
-    def __init__(self, buf, send, recv, pos, peers):
-        self.buf, self.send, self.recv = buf, send, recv
-        self.yh, self.z, self.c = pos
+    eager = True
+
+    def __init__(self, buf, cols, send, recv, base, pos, peers):
+        self.buf, self.cols = buf, cols
+        self.send, self.recv, self.base = send, recv, base
+        self.yl, self.yh, self.z, self.c = pos
         self.peers = peers
         self.sent = []
 
-    def block(self, yh, z):
-        return self.buf.at[yh, z, self.c]
-
-    def push(self, ref, i, peer):
-        copy = pltpu.make_async_remote_copy(
+    def block(self, yh, off, full=False, other=False):
+        ref = self.buf.at[yh, lax.rem(self.z + off, ZG), 1 - self.c if other else self.c]
+        return ref if full else ref.at[:, self.cols]
+
+    def slot(self, k, yl):
+        return yl * (0, 2, 6, 4)[k] + (1 - yl) * (1, 7, 3, 5)[k]
+
+    def copy(self, ref, i, peer):
+        i = self.base + i
+        return pltpu.make_async_remote_copy(
             src_ref=ref, dst_ref=ref, send_sem=self.send.at[i], recv_sem=self.recv.at[i],
             device_id=self.peers[peer], device_id_type=MESH,
         )
+
+    def push(self, ref, i, peer):
+        copy = self.copy(ref, i, peer)
         copy.start()
         self.sent.append(copy)
 
     def arrive(self, ref, i, peer):
-        pltpu.make_async_remote_copy(
-            src_ref=ref, dst_ref=ref, send_sem=self.send.at[i], recv_sem=self.recv.at[i],
-            device_id=self.peers[peer], device_id_type=MESH,
-        ).wait_recv()
+        self.copy(ref, i, peer).wait_recv()
+
+    def give(self, yh, off, i):
+        self.push(self.block(yh, off), i, "core")
 
     def own(self):
-        mine = self.block(self.yh, self.z)
+        mine = self.block(self.yh, 0)
         self.push(mine, 0, "z+")
         self.push(mine, 4, "z-")
-        self.push(mine, 7, "part")
+        self.give(self.yh, 0, 15)
 
     def step(self, s):
-        low = self.block(self.yh, lax.rem(self.z + ZG - s, ZG))
+        low = self.block(self.yh, ZG - s)
         self.arrive(low, s - 1, "z+")
         if s < 4:
             self.push(low, s, "z+")
-        self.push(low, 7 + s, "part")
-        if s < 4:
-            high = self.block(self.yh, lax.rem(self.z + s, ZG))
+            high = self.block(self.yh, s)
             self.arrive(high, 3 + s, "z-")
             if s < 3:
                 self.push(high, 4 + s, "z-")
-            self.push(high, 11 + s, "part")
-
-    def share_own(self):
-        self.push(self.buf.at[self.yh, :, self.c], 15, "core")
-
-    def share_other(self):
-        other = 1 - self.yh
-        self.arrive(self.block(other, self.z), 7, "part")
-        for s in range(1, 5):
-            self.arrive(self.block(other, lax.rem(self.z + ZG - s, ZG)), 7 + s, "part")
-            if s < 4:
-                self.arrive(self.block(other, lax.rem(self.z + s, ZG)), 11 + s, "part")
-        self.push(self.buf.at[other, :, self.c], 16, "core")
+        if self.eager:
+            self.push(self.block(self.yh, self.slot(s - 1, self.yl)), 6 + s, "part")
+        self.give(self.yh, ZG - s, 15 + ZG - s)
+        if s < 4:
+            self.give(self.yh, s, 15 + s)
+
+    def relay(self, k):
+        off = self.slot(k, 1 - self.yl)
+        self.arrive(self.block(1 - self.yh, off), 7 + k, "part")
+        self.push(self.block(1 - self.yh, off), 11 + k, "low")
+        self.give(1 - self.yh, off, 23 + k)
+
+    def collect(self, k):
+        off = self.slot(k, self.yl)
+        self.arrive(self.block(1 - self.yh, off), 11 + k, "low")
+        self.give(1 - self.yh, off, 27 + k)
 
     def shared(self):
-        self.arrive(self.buf.at[self.yh, :, 1 - self.c], 15, "core")
-        self.arrive(self.buf.at[1 - self.yh, :, 1 - self.c], 16, "core")
+        for off in range(ZG):
+            self.arrive(self.block(self.yh, off, other=True), 15 + off, "core")
+        for k in range(4):
+            for i, yl in ((23, 1 - self.yl), (27, self.yl)):
+                off = self.slot(k, yl)
+                self.arrive(self.block(1 - self.yh, off, other=True), i + k, "core")
 
     def finish(self):
         for copy in self.sent:
             copy.wait_send()
+
+
+class WideRing(Ring):
+    eager = False
+
+    def part(self, k):
+        self.push(self.block(self.yh, self.slot(k, self.yl)), 7 + k, "part")
+
+    def give(self, yh, off, i):
+        pass
+
+    def whole(self, yh, c, other=False):
+        return self.buf.at[yh, :, c, :, self.rest if other else self.cols]
+
+    def swap(self):
+        self.push(self.whole(self.yh, self.c), 15, "x+")
+        self.push(self.whole(1 - self.yh, self.c), 16, "x-")
+        self.push(self.whole(self.yh, self.c), 17, "core")
+        self.push(self.whole(1 - self.yh, self.c), 18, "core")
+
+    def swapped(self):
+        self.arrive(self.whole(self.yh, self.c, True), 15, "x+")
+        self.push(self.whole(self.yh, self.c, True), 19, "core")
+        self.arrive(self.whole(1 - self.yh, self.c, True), 16, "x-")
+        self.push(self.whole(1 - self.yh, self.c, True), 20, "core")
+
+    def shared(self):
+        c = 1 - self.c
+        self.arrive(self.whole(self.yh, c), 17, "core")
+        self.arrive(self.whole(1 - self.yh, c), 18, "core")
+        self.arrive(self.whole(self.yh, c, True), 19, "core")
+        self.arrive(self.whole(1 - self.yh, c, True), 20, "core")
 
 
 def kernel(
@@ -122,12 +170,26 @@
         "z-": {"tm": tm, "tok": yh * 2 * ZG + lax.rem(z + ZG - 1, ZG) * 2 + c},
         "core": {"tm": tm, "tok": yh * 2 * ZG + z * 2 + 1 - c},
         "part": {"tm": (1 - yl) * XG + x, "tok": (1 - yh) * 2 * ZG + z * 2 + c},
+        "low": {"tm": (1 - yl) * XG + x, "tok": tok},
+        "x+": at_x(1),
+        "x-": at_x(3),
     }
-    lower = {"tm": (1 - yl) * XG + x, "tok": tok}
+    lower = peers["low"]
     beside = at_tok(2 * c - 1)
 
+    own_copies = []
+    for j in range(3):
+        column = pl.multiple_of(j * width + x * CW, HD)
+        own_copies.append(pltpu.make_async_copy(
+            wqkv_ref.at[:, pl.ds(column, CW)],
+            wbuf.at[yh, z, c, :, pl.ds((j + 2) % 3 * CW, CW)], lsem.at[j],
+        ))
+    own_copies.append(pltpu.make_async_copy(wout_ref, wo.at[yh, z, c], lsem.at[3]))
+    for copy in own_copies:
+        copy.start()
+
     barrier = pltpu.get_barrier_semaphore()
-    everyone = [at_x(1), at_x(2), at_x(3), *peers.values(), lower, beside]
+    everyone = [at_x(2), *peers.values(), beside]
     for peer in everyone:
         pl.semaphore_signal(barrier, inc=1, device_id=peer, device_id_type=MESH)
     pl.semaphore_wait(barrier, len(everyone))
@@ -147,25 +209,25 @@
 
     top, bottom = pl.ds(0, part_rows), pl.ds(part_rows, part_rows)
 
-    own_copies = []
-    for j in range(3):
-        column = pl.multiple_of(j * width + x * CW, HD)
-        own_copies.append(pltpu.make_async_copy(
-            wqkv_ref.at[:, pl.ds(column, CW)],
-            wbuf.at[yh, z, c, :, pl.ds(j * CW, CW)], lsem.at[j],
-        ))
-    own_copies.append(pltpu.make_async_copy(wout_ref, wo.at[yh, z, c], lsem.at[3]))
-    for copy in own_copies:
-        copy.start()
-
     push(h_ref.at[top], hbuf.at[0, top], hs, hr, 0, at_x(1))
     push(h_ref.at[bottom], hbuf.at[0, bottom], hs, hr, 1, at_x(3))
     for copy in own_copies:
         copy.wait()
-    pos = (yh, z, c)
-    wring = Ring(wbuf, ws, wr, pos, peers)
-    oring = Ring(wo, os, orecv, pos, peers)
-    wring.own()
+    pos = (yl, yh, z, c)
+    cut = 2 * CW
+    wfirst = Ring(wbuf, pl.ds(0, cut), ws, wr, 0, pos, peers)
+    wlast = Ring(wbuf, pl.ds(cut, 3 * CW - cut), ws, wr, 31, pos, peers)
+    parity = lax.rem(x, 2)
+    span = width // 2
+
+    def wide(i):
+        return pl.ds(pl.multiple_of(i * span, HD), span)
+
+    oring = WideRing(wo, wide(parity), os, orecv, 0, pos, peers)
+    oring.rest = wide(1 - parity)
+    wfirst.own()
+    wlast.own()
+    oring.own()
     push(h_ref.at[bottom], hbuf.at[1, top], hs, hr, 2, at_x(1))
     push(h_ref.at[top], hbuf.at[1, bottom], hs, hr, 3, at_x(3))
 
@@ -174,23 +236,51 @@
         remote(hbuf.at[group, top], hbuf.at[group, top], hs, hr, i, at_x(1)).wait_recv()
         remote(hbuf.at[group, bottom], hbuf.at[group, bottom], hs, hr, i + 1, at_x(3)).wait_recv()
 
-    wring.step(1)
-    wring.step(2)
-    wring.step(3)
+    wfirst.step(1)
+    wlast.step(1)
+    oring.step(1)
+    oring.part(0)
+    wfirst.step(2)
+    wlast.step(2)
+    wfirst.relay(0)
+    wlast.relay(0)
+    oring.step(2)
+    oring.part(1)
+    wfirst.step(3)
+    wlast.step(3)
     h_arrive(0)
     push(hbuf.at[0, top], hbuf.at[2, top], hs, hr, 4, at_x(1))
     push(hbuf.at[0, bottom], hbuf.at[2, bottom], hs, hr, 5, at_x(3))
-    wring.step(4)
-    wring.share_own()
-    oring.own()
-    oring.step(1)
-    oring.step(2)
-    wring.share_other()
-    wring.shared()
+    wfirst.relay(1)
+    wlast.relay(1)
+    wfirst.collect(0)
+    wlast.collect(0)
+    oring.step(3)
+    oring.part(2)
+    oring.relay(0)
+    wfirst.step(4)
+    wlast.step(4)
+    wfirst.relay(2)
+    wlast.relay(2)
+    wfirst.collect(1)
+    wlast.collect(1)
+    oring.step(4)
+    oring.part(3)
+    oring.relay(1)
+    wfirst.relay(3)
+    wlast.relay(3)
+    oring.relay(2)
+    wfirst.collect(2)
+    wlast.collect(2)
+    oring.collect(0)
+    wfirst.collect(3)
+    wlast.collect(3)
+    oring.relay(3)
+    wfirst.shared()
 
     kvs = (kv0, kv1, kv2, kv3)
 
-    def qkv(group):
+    def project(group, first, last):
         kv = kvs[group]
 
         def one(j, carry):
@@ -202,22 +292,48 @@
             for head in range(HL):
                 piece = part[:, head * HD : (head + 1) * HD]
                 norm = lax.rsqrt(jnp.mean(piece * piece, -1, keepdims=True) + 1e-06)
-                pieces.append(piece * jnp.where(j < 2, norm, 1.0))
+                pieces.append(piece * jnp.where(j == 1, 1.0, norm))
             done = jnp.concatenate(pieces, axis=1).astype(jnp.bfloat16)
             for half in range(2):
                 for tile in range(2):
-                    first = half * part_rows + tile * TILE
-                    kv[2 + tile, j, half] = done[first : first + TILE]
+                    row = half * part_rows + tile * TILE
+                    kv[2 + tile, j, half] = done[row : row + TILE]
             return carry
 
-        lax.fori_loop(0, 3, one, 0)
-        push(kv.at[2:4, 1:3], kv.at[0:2, 1:3], ks, kr, 2 * group, at_tok(1))
-        push(kv.at[2:4, 1:3], kv.at[4:6, 1:3], ks, kr, 2 * group + 1, at_tok(-1))
+        lax.fori_loop(first, last, one, 0)
+
+    def halo(group):
+        kv = kvs[group]
+        mine = kv.at[2:4, 0:2]
+        return (
+            remote(mine, kv.at[0:2, 0:2], ks, kr, 2 * group, at_tok(1)),
+            remote(mine, kv.at[4:6, 0:2], ks, kr, 2 * group + 1, at_tok(-1)),
+        )
+
+    def keys_values(group):
+        project(group, 0, 2)
+        ahead, behind = halo(group)
+
+        @pl.when(tok < ntok - 1)
+        def _():
+            ahead.start()
+
+        @pl.when(tok > 0)
+        def _():
+            behind.start()
 
     def attend(group):
         kv = kvs[group]
-        remote(kv.at[0:2, 1:3], kv.at[0:2, 1:3], ks, kr, 2 * group, at_tok(1)).wait_recv()
-        remote(kv.at[4:6, 1:3], kv.at[4:6, 1:3], ks, kr, 2 * group + 1, at_tok(-1)).wait_recv()
+        ahead, behind = halo(group)
+
+        @pl.when(tok > 0)
+        def _():
+            ahead.wait_recv()
+
+        @pl.when(tok < ntok - 1)
+        def _():
+            behind.wait_recv()
+
 
         def one(i, carry):
             half, tile = lax.div(i, 2), lax.rem(i, 2)
@@ -233,9 +349,9 @@
             near = [
                 jnp.clip(nb_ref[tile, n] - (2 * tok - 2), 0, 5) for n in range(nb_ref.shape[1])
             ]
-            query = kv[2 + tile, 0, half]
-            keys = jnp.concatenate([kv[n, 1, half] for n in near], axis=0)
-            values = jnp.concatenate([kv[n, 2, half] for n in near], axis=0)
+            query = kv[2 + tile, 2, half]
+            keys = jnp.concatenate([kv[n, 0, half] for n in near], axis=0)
+            values = jnp.concatenate([kv[n, 1, half] for n in near], axis=0)
             outs = []
             for head in range(HL):
                 cols = slice(head * HD, (head + 1) * HD)
@@ -254,19 +370,25 @@
             )
             return carry
 
-        lax.fori_loop(0, 4, one, 0)
-
-    qkv(0)
-    oring.step(3)
-    qkv(1)
-    oring.step(4)
-    oring.share_own()
+        lax.fori_loop(0, 4, one, 0, unroll=2)
+
+    keys_values(0)
+    keys_values(1)
+    h_arrive(1)
+    keys_values(2)
+    h_arrive(2)
+    keys_values(3)
+    wlast.shared()
+    project(0, 2, 3)
+    project(1, 2, 3)
+    project(2, 2, 3)
+    project(3, 2, 3)
+    oring.collect(1)
+    oring.collect(2)
+    oring.collect(3)
+    oring.swap()
     attend(0)
-    h_arrive(1)
-    qkv(2)
     attend(1)
-    h_arrive(2)
-    qkv(3)
     attend(2)
     attend(3)
 
@@ -289,7 +411,7 @@
         push(sbuf.at[pl.ds(2 * lax.rem(x + k, XG), 2)], columns_of(x), ss, sr, k - 1, at_x(k))
     keep = pltpu.make_async_copy(sbuf.at[pl.ds(2 * x, 2)], columns_of(x), lsem.at[4])
     keep.start()
-    oring.share_other()
+    oring.swapped()
     oring.shared()
     keep.wait()
     for k in range(1, XG):
@@ -309,8 +431,20 @@
         return carry
 
     lax.fori_loop(0, width // chunk, finish, 0)
-    wring.finish()
+    wfirst.finish()
+    wlast.finish()
     oring.finish()
+    for group in range(4):
+        ahead, behind = halo(group)
+
+        @pl.when(tok < ntok - 1)
+        def _():
+            ahead.wait_send()
+
+        @pl.when(tok > 0)
+        def _():
+            behind.wait_send()
+
     for copy in sent:
         copy.wait_send()
 
@@ -350,8 +484,8 @@
             pltpu.VMEM((steps_here, tok_here, width), bf),
             dma((5,)),
             dma((6,)), dma((6,)),
-            dma((17,)), dma((17,)),
-            dma((17,)), dma((17,)),
+            dma((62,)), dma((62,)),
+            dma((21,)), dma((21,)),
             dma((8,)), dma((8,)),
             dma((1,)), dma((1,)),
             dma((3,)), dma((3,)),

time: 98.5 us -> 86.7 us (0.88)
  Pallas kernels: 89.4 us -> 77.6 us
    pallas_call x1, Pallas kernels: 89.4 us -> 77.6 us  [body(): pl.pallas_call(kernel, out_shape=jax.ShapeDtypeStruct((steps_here, tok_he...]
where the time goes in v2:
time: 86.7 us; the launch traced here: 86.5 us
  Pallas kernels  77.6 us (90%)
  other arithmetic  5.2 us (6%)
  local copies, waits for them, and re-layouts  3.28 us (4%)
    pallas_call x1, Pallas kernels, body(): pl.pallas_call(kernel, out_shape=jax.ShapeDtypeStruct((steps_here, tok_he...  77.6 us
    unnamed x5, local copies, waits for them, and re-layouts  2.66 us

profile of v2, /device:TPU:32, one launch (start us, length us, event | category | flops | bytes accessed | tf_op | source)
XLA Modules:
  0.0 86.5 jit_solution(6922440742045434154)
XLA Ops:
  0.0 0.0 copy-start
  0.0 0.8 convert_multiply_fusion
  0.8 0.1 dynamic-slice_multiply_fusion
  0.9 0.1 slice_subtract_fusion
  0.9 0.6 dynamic-slice_bitcast_fusion.step_ref
  1.6 0.0 copy-start.1
  1.6 1.4 %convert_reduce_fusion = f32[2,128]{1,0:T(2,128)S(1)} fusion(bf16[2,128,1536]{2,1,0:T(8,128)(2,1)} %param.8), kind=kLoop, calls=%fused_computation.1 | loop fusion | flops 786176 | bytes 787456 | tf_op jit(solution)/shard_map/reduce_sum | solution.py:32
  3.0 1.5 %fusion.2 = f32[2,128]{1,0:T(2,128)S(1)} fusion(bf16[2,128,1536]{2,1,0:T(8,128)(2,1)} %param.8, f32[2,128]{1,0:T(2,128)S(1)} %broadcast_multiply_fusion), kind=kLoop, calls=%fused_computation.4 | loop fusion | flops 1572608 | bytes 788480 | tf_op jit(solution)/shard_map/reduce_sum | solution.py:33
  4.5 0.1 multiply_cosine_fusion
  4.6 0.0 copy-done
  4.6 0.3 fusion.7
  4.9 0.0 copy-done.1
  4.9 1.3 %fusion.5 = bf16[2,128,1536]{2,1,0:T(8,128)(2,1)} fusion(bf16[2,128,1536]{2,1,0:T(8,128)(2,1)S(1)} %copy-done.1, f32[2,1536]{1,0:T(2,128)S(1)} %get-tuple-element.6, f32[2,1536]{1,0:T(2,128)S(1)} %get-tuple-element.5, f32[2,128]{1,0:T(2,128)S(1)} %add_sqrt_fusion, f32[2,128]{1,0:T(2,128)S(1)} %broadcast_multiply_fusion), kind=kLoop, calls=%fused_computation.7 | loop fusion | flops 2359296 | bytes 1599488 | tf_op jit(solution)/shard_map/convert_element_type | solution.py:34
  6.2 77.6 %shard_map.73 = f32[2,128,1536]{2,1,0:T(8,128)} custom-call(bf16[256,1536]{1,0:T(8,128)(2,1)} %bitcast.4, bf16[48,4608]{1,0:T(8,128)(2,1)} %wqkv_ref.1, bf16[48,1536]{1,0:T(8,128)(2,1)} %wout_ref.1, bf16[128,1536]{1,0:T(8,128)(2,1)} %start_ref.1, s32[2,3]{1,0:T(2,128)} %nb_ref.1, f32[1,8]{1,0:T(1,128)} %dynamic-slice_bitcast_fusion.step_ref), custom_call_target="tpu_custom_call" | custom-call | tf_op jit(solution)/shard_map/pallas_call | solution.py:470
  83.8 2.7 %copy.9 = f32[2,128,1536]{2,1,0:T(8,128)} copy(f32[2,128,1536]{2,1,0:T(8,128)} %shard_map.73) | data formatting | bytes 3145728
  (4 shorter events, 0.0 us)
Async XLA Ops:
  0.0 4.6 %copy-start = (bf16[256,3072]{1,0:T(8,128)(2,1)S(1)}, bf16[256,3072]{1,0:T(8,128)(2,1)}, u32[]{:S(2)}) copy-start(bf16[256,3072]{1,0:T(8,128)(2,1)} %param.11) | copy-start | bytes 4718596
  1.6 3.4 %copy-start.1 = (bf16[2,128,1536]{2,1,0:T(8,128)(2,1)S(1)}, bf16[2,128,1536]{2,1,0:T(8,128)(2,1)}, u32[]{:S(2)}) copy-start(bf16[2,128,1536]{2,1,0:T(8,128)(2,1)} %param.8) | copy-start | bytes 2359300

commit v3 on v2

--- a/solution.py
+++ b/solution.py
@@ -1,4 +1,3 @@
-import functools
 import math
 
 import jax
@@ -16,22 +15,6 @@
 CW = HL * HD
 TILE = 64
 MESH = pl.DeviceIdType.MESH
-
-
-def time_mod(times, mod_weight):
-    half = mod_weight.shape[0] // 2
-    freqs = jnp.exp(-math.log(10000.0) * jnp.arange(half, dtype=jnp.float32) / half)
-    angle = 1000.0 * times[:, None] * freqs[None, :]
-    embed = jnp.concatenate([jnp.cos(angle), jnp.sin(angle)], axis=1)
-    act = jax.nn.silu(embed).astype(jnp.bfloat16)
-    return jnp.dot(act, mod_weight, preferred_element_type=jnp.float32)
-
-
-def modulate(state, shift, scale):
-    values = state.astype(jnp.float32)
-    center = values - jnp.mean(values, -1, keepdims=True)
-    spread = jnp.mean(center * center, -1, keepdims=True)
-    return (center / jnp.sqrt(spread + 1e-06) * (1.0 + scale) + shift).astype(jnp.bfloat16)
 
 
 class Ring:
@@ -147,16 +130,15 @@
 
 
 def kernel(
-    h_ref, wqkv_ref, wout_ref, start_ref, nb_ref, step_ref, out_ref,
-    hbuf, wbuf, wo, kv0, kv1, kv2, kv3, abuf, tsend, trecv, sbuf, sall,
+    x_ref, plan_ref, freq_ref, mod_ref, wqkv_ref, wout_ref, start_hbm, nb_ref, out_ref,
+    start_ref, own, modw, mods, hbuf, hnorm, wbuf, wo, kv0, kv1, kv2, kv3, abuf, tsend, trecv, sbuf, sall,
     lsem, hs, hr, ws, wr, os, orecv, ks, kr, ts, tr, ss, sr,
 ):
     tm, tok = lax.axis_index("tm"), lax.axis_index("tok")
     x, yl = lax.rem(tm, XG), lax.div(tm, XG)
     yh, z, c = lax.div(tok, 2 * ZG), lax.div(lax.rem(tok, 2 * ZG), 2), lax.rem(tok, 2)
-    width = h_ref.shape[1]
-    rows = h_ref.shape[0]
-    part_rows = rows // 2
+    part_rows, width = x_ref.shape[1:]
+    rows = 2 * part_rows
     ntok = 4 * ZG
 
     def at_x(k):
@@ -185,7 +167,12 @@
             wbuf.at[yh, z, c, :, pl.ds((j + 2) % 3 * CW, CW)], lsem.at[j],
         ))
     own_copies.append(pltpu.make_async_copy(wout_ref, wo.at[yh, z, c], lsem.at[3]))
-    for copy in own_copies:
+    state_copies = [
+        pltpu.make_async_copy(x_ref, own, lsem.at[5]),
+        pltpu.make_async_copy(mod_ref, modw, lsem.at[6]),
+        pltpu.make_async_copy(start_hbm, start_ref, lsem.at[7]),
+    ]
+    for copy in own_copies + state_copies:
         copy.start()
 
     barrier = pltpu.get_barrier_semaphore()
@@ -209,8 +196,8 @@
 
     top, bottom = pl.ds(0, part_rows), pl.ds(part_rows, part_rows)
 
-    push(h_ref.at[top], hbuf.at[0, top], hs, hr, 0, at_x(1))
-    push(h_ref.at[bottom], hbuf.at[0, bottom], hs, hr, 1, at_x(3))
+    push(x_ref.at[0], hbuf.at[0, top], hs, hr, 0, at_x(1))
+    push(x_ref.at[1], hbuf.at[0, bottom], hs, hr, 1, at_x(3))
     for copy in own_copies:
         copy.wait()
     pos = (yl, yh, z, c)
@@ -228,14 +215,62 @@
     wfirst.own()
     wlast.own()
     oring.own()
-    push(h_ref.at[bottom], hbuf.at[1, top], hs, hr, 2, at_x(1))
-    push(h_ref.at[top], hbuf.at[1, bottom], hs, hr, 3, at_x(3))
+    push(x_ref.at[1], hbuf.at[1, top], hs, hr, 2, at_x(1))
+    push(x_ref.at[0], hbuf.at[1, bottom], hs, hr, 3, at_x(3))
 
     def h_arrive(group):
         i = 2 * group
         remote(hbuf.at[group, top], hbuf.at[group, top], hs, hr, i, at_x(1)).wait_recv()
         remote(hbuf.at[group, bottom], hbuf.at[group, bottom], hs, hr, i + 1, at_x(3)).wait_recv()
 
+    def timestep(group, half):
+        if group == 0:
+            return 2 * x + half
+        if group == 3:
+            return 2 * lax.rem(x + 2, XG) + half
+        owner = lax.rem(x + 3 + 2 * half, XG)
+        return 2 * owner + (half if group == 1 else 1 - half)
+
+    def plan_row(k, shape):
+        return jnp.full(shape, plan_ref[yl * 2 * XG + k].astype(jnp.float32)) / NSCHED
+
+    def time_of(k):
+        return plan_row(k, (1, HD))
+
+    def modulation():
+        times = jnp.concatenate([plan_row(k, (1, freq_ref.shape[1])) for k in range(2 * XG)], axis=0)
+        angle = 1000.0 * times * freq_ref[...]
+        embed = jnp.concatenate([jnp.cos(angle), jnp.sin(angle)], axis=1)
+        act = (embed / (1.0 + jnp.exp(-embed))).astype(jnp.bfloat16)
+        mods[...] = jnp.dot(act, modw[...], preferred_element_type=jnp.float32)
+
+    band = 16
+
+    def norm(group):
+        def one(i, carry):
+            half, row = lax.div(i, part_rows // band), lax.rem(i, part_rows // band) * band
+            at = pl.ds(pl.multiple_of(row, band), band)
+            if group == 0:
+                values = own[half, at, :]
+            else:
+                at_row = pl.multiple_of(i * band, band)
+                values = hbuf[group - 1, pl.ds(at_row, band), :]
+            values = values.astype(jnp.float32)
+            when = timestep(group, half)
+            shift = mods[pl.ds(when, 1), :width]
+            scale = mods[pl.ds(when, 1), width:]
+            center = values - jnp.mean(values, -1, keepdims=True)
+            spread = jnp.mean(center * center, -1, keepdims=True)
+            done = center * lax.rsqrt(spread + 1e-06) * (1.0 + scale) + shift
+            hnorm[group, pl.ds(pl.multiple_of(i * band, band), band), :] = done.astype(jnp.bfloat16)
+            return carry
+
+        lax.fori_loop(0, rows // band, one, 0, unroll=4)
+
+    for copy in state_copies:
+        copy.wait()
+    modulation()
+    norm(0)
     wfirst.step(1)
     wlast.step(1)
     oring.step(1)
@@ -251,6 +286,7 @@
     h_arrive(0)
     push(hbuf.at[0, top], hbuf.at[2, top], hs, hr, 4, at_x(1))
     push(hbuf.at[0, bottom], hbuf.at[2, bottom], hs, hr, 5, at_x(3))
+    norm(1)
     wfirst.relay(1)
     wlast.relay(1)
     wfirst.collect(0)
@@ -270,6 +306,8 @@
     wfirst.relay(3)
     wlast.relay(3)
     oring.relay(2)
+    h_arrive(1)
+    norm(2)
     wfirst.collect(2)
     wlast.collect(2)
     oring.collect(0)
@@ -285,7 +323,7 @@
 
         def one(j, carry):
             column = pl.multiple_of(j * CW, HD)
-            left = h_ref[...] if group == 0 else hbuf[group - 1]
+            left = hnorm[group]
             right = wbuf[:, :, :, :, pl.ds(column, CW)].reshape(width, CW)
             part = jnp.dot(left, right, preferred_element_type=jnp.float32)
             pieces = []
@@ -302,50 +340,46 @@
 
         lax.fori_loop(first, last, one, 0)
 
-    def halo(group):
+    def halo(group, j):
+        mine = kvs[group].at[2:4, j]
+        i = 4 * group + 2 * j
+        return (
+            remote(mine, kvs[group].at[0:2, j], ks, kr, i, at_tok(1)),
+            remote(mine, kvs[group].at[4:6, j], ks, kr, i + 1, at_tok(-1)),
+        )
+
+    def keys_values(group):
+        for j in range(2):
+            project(group, j, j + 1)
+            ahead, behind = halo(group, j)
+
+            @pl.when(tok < ntok - 1)
+            def _():
+                ahead.start()
+
+            @pl.when(tok > 0)
+            def _():
+                behind.start()
+
+    def attend(group):
         kv = kvs[group]
-        mine = kv.at[2:4, 0:2]
-        return (
-            remote(mine, kv.at[0:2, 0:2], ks, kr, 2 * group, at_tok(1)),
-            remote(mine, kv.at[4:6, 0:2], ks, kr, 2 * group + 1, at_tok(-1)),
-        )
-
-    def keys_values(group):
-        project(group, 0, 2)
-        ahead, behind = halo(group)
+        copies = [halo(group, j) for j in range(2)]
+
+        @pl.when(tok > 0)
+        def _():
+            for ahead, _ in copies:
+                ahead.wait_recv()
 
         @pl.when(tok < ntok - 1)
         def _():
-            ahead.start()
-
-        @pl.when(tok > 0)
-        def _():
-            behind.start()
-
-    def attend(group):
-        kv = kvs[group]
-        ahead, behind = halo(group)
-
-        @pl.when(tok > 0)
-        def _():
-            ahead.wait_recv()
-
-        @pl.when(tok < ntok - 1)
-        def _():
-            behind.wait_recv()
+            for _, behind in copies:
+                behind.wait_recv()
 
 
         def one(i, carry):
             half, tile = lax.div(i, 2), lax.rem(i, 2)
-            if group == 0:
-                when = 2 * x + half
-            elif group == 3:
-                when = 2 * lax.rem(x + 2, XG) + half
-            elif group == 1:
-                when = 2 * lax.rem(x + 3 + 2 * half, XG) + half
-            else:
-                when = 2 * lax.rem(x + 3 + 2 * half, XG) + 1 - half
-            step = step_ref[0, when]
+            when = timestep(group, half)
+            step = time_of(when) - time_of(when + 1)
             near = [
                 jnp.clip(nb_ref[tile, n] - (2 * tok - 2), 0, 5) for n in range(nb_ref.shape[1])
             ]
@@ -370,13 +404,13 @@
             )
             return carry
 
-        lax.fori_loop(0, 4, one, 0, unroll=2)
+        lax.fori_loop(0, 4, one, 0, unroll=4)
 
     keys_values(0)
     keys_values(1)
-    h_arrive(1)
     keys_values(2)
     h_arrive(2)
+    norm(3)
     keys_values(3)
     wlast.shared()
     project(0, 2, 3)
@@ -407,42 +441,59 @@
     def columns_of(src):
         return sall.at[:, :, pl.ds(pl.multiple_of(src * CW, HD), CW)]
 
-    for k in range(1, XG):
+    for k in (1, 3, 2):
         push(sbuf.at[pl.ds(2 * lax.rem(x + k, XG), 2)], columns_of(x), ss, sr, k - 1, at_x(k))
     keep = pltpu.make_async_copy(sbuf.at[pl.ds(2 * x, 2)], columns_of(x), lsem.at[4])
     keep.start()
     oring.swapped()
     oring.shared()
     keep.wait()
-    for k in range(1, XG):
+
+    def s_arrive(k):
         source = columns_of(lax.rem(x + XG - k, XG))
         remote(source, source, ss, sr, k - 1, at_x(k)).wait_recv()
 
     chunk = 256
 
-    def finish(i, carry):
-        column = pl.ds(pl.multiple_of(i * chunk, chunk), chunk)
-        left = sall[...].reshape(rows, width)
-        right = wo[:, :, :, :, column].reshape(width, chunk)
-        before = jnp.dot(left, right, preferred_element_type=jnp.float32)
-        first = start_ref[:, column].astype(jnp.float32)
-        out_ref[0, :, column] = first - before[:part_rows]
-        out_ref[1, :, column] = first - before[part_rows:]
-        return carry
-
-    lax.fori_loop(0, width // chunk, finish, 0)
+    def finish(near):
+        def one(i, carry):
+            column = pl.ds(pl.multiple_of(i * chunk, chunk), chunk)
+            before = 0.0
+            for k in (0, 1, 3) if near else (2,):
+                src = lax.rem(x + k, XG)
+                left = sall[:, :, pl.ds(pl.multiple_of(src * CW, HD), CW)].reshape(rows, CW)
+                part = pl.ds(lax.rem(src, 2) * (ZG // 2), ZG // 2)
+                right = wo[lax.div(src, 2), part, :, :, column].reshape(CW, chunk)
+                before = before + jnp.dot(left, right, preferred_element_type=jnp.float32)
+            for half in range(2):
+                done = before[half * part_rows : (half + 1) * part_rows]
+                if near:
+                    first = start_ref[:, column].astype(jnp.float32)
+                else:
+                    first = out_ref[half, :, column]
+                out_ref[half, :, column] = first - done
+            return carry
+
+        lax.fori_loop(0, width // chunk, one, 0)
+
+    s_arrive(1)
+    s_arrive(3)
+    finish(True)
+    s_arrive(2)
+    finish(False)
     wfirst.finish()
     wlast.finish()
     oring.finish()
-    for group in range(4):
-        ahead, behind = halo(group)
-
-        @pl.when(tok < ntok - 1)
-        def _():
+    copies = [halo(group, j) for group in range(4) for j in range(2)]
+
+    @pl.when(tok < ntok - 1)
+    def _():
+        for ahead, _ in copies:
             ahead.wait_send()
 
-        @pl.when(tok > 0)
-        def _():
+    @pl.when(tok > 0)
+    def _():
+        for _, behind in copies:
             behind.wait_send()
 
     for copy in sent:
@@ -452,28 +503,26 @@
 def body(start, trajectory, plan, neighbors, mod_weight, w_qkv, w_out):
     steps_here, tok_here, width = trajectory.shape
     rows = steps_here * tok_here
-    times = plan.astype(jnp.float32) / NSCHED
-    steps = times[:-1] - times[1:]
-    tm = lax.axis_index("tm")
-    own_times = lax.dynamic_slice_in_dim(times, tm * steps_here, steps_here)
-    ring_steps = lax.dynamic_slice_in_dim(
-        steps, lax.div(tm, XG) * XG * steps_here, XG * steps_here
-    )[None]
-    mod = time_mod(own_times, mod_weight)
-    h = modulate(trajectory, mod[:, None, :width], mod[:, None, width:]).reshape(rows, width)
+    half = mod_weight.shape[0] // 2
+    freqs = jnp.exp(-math.log(10000.0) * jnp.arange(half, dtype=jnp.float32) / half)[None]
     bf, f32 = jnp.bfloat16, jnp.float32
     kv = pltpu.VMEM((6, 3, steps_here, TILE, CW), bf)
     dma = pltpu.SemaphoreType.DMA
     vmem = pl.BlockSpec(memory_space=pltpu.VMEM)
     smem = pl.BlockSpec(memory_space=pltpu.SMEM)
-    hbm = pl.BlockSpec(memory_space=pl.ANY)
+    hbm = pl.BlockSpec(memory_space=pltpu.HBM)
     return pl.pallas_call(
         kernel,
-        out_shape=jax.ShapeDtypeStruct((steps_here, tok_here, width), f32),
-        in_specs=[vmem, hbm, hbm, vmem, smem, smem],
+        out_shape=pltpu.VMEM((steps_here, tok_here, width), f32),
+        in_specs=[hbm, smem, vmem, hbm, hbm, hbm, hbm, smem],
         out_specs=vmem,
         scratch_shapes=[
+            pltpu.VMEM((tok_here, width), bf),
+            pltpu.VMEM((steps_here, tok_here, width), bf),
+            pltpu.VMEM(mod_weight.shape, bf),
+            pltpu.VMEM((2 * XG, 2 * width), f32),
             pltpu.VMEM((3, rows, width), bf),
+            pltpu.VMEM((4, rows, width), bf),
             pltpu.VMEM((2, ZG, 2, w_qkv.shape[0], 3 * CW), bf),
             pltpu.VMEM((2, ZG, 2, w_out.shape[0], width), bf),
             kv, kv, kv, kv,
@@ -482,16 +531,18 @@
             pltpu.VMEM((tok_here, CW), bf),
             pltpu.VMEM((2 * XG, tok_here, CW), bf),
             pltpu.VMEM((steps_here, tok_here, width), bf),
-            dma((5,)),
+            dma((8,)),
             dma((6,)), dma((6,)),
             dma((62,)), dma((62,)),
             dma((21,)), dma((21,)),
-            dma((8,)), dma((8,)),
+            dma((16,)), dma((16,)),
             dma((1,)), dma((1,)),
             dma((3,)), dma((3,)),
         ],
-        compiler_params=pltpu.CompilerParams(collective_id=0, has_side_effects=True),
-    )(h, w_qkv, w_out, start, neighbors, ring_steps)
+        compiler_params=pltpu.CompilerParams(
+            collective_id=0, has_side_effects=True, vmem_limit_bytes=56 << 20
+        ),
+    )(trajectory, plan, freqs, mod_weight, w_qkv, w_out, start, neighbors)
 
 
 def solution(mesh):

time: 86.7 us -> 77.5 us (0.89)
  other arithmetic: 5.2 us -> 0.52 us
  Pallas kernels: 77.6 us -> 74.7 us
  local copies, waits for them, and re-layouts: 3.28 us -> 1.15 us
    pallas_call x1, Pallas kernels: 77.6 us -> 74.7 us  [body(): pl.pallas_call(kernel, out_shape=pltpu.VMEM((steps_here, tok_here, width)...]
    reduce_sum x2 -> x0, other arithmetic: 2.87 us -> none  [the longest x1 1.48 us: modulate(): spread = jnp.mean(center * center, -1, keepdims=True)]
    unnamed x5 -> x1, local copies, waits for them, and re-layouts: 2.66 us -> 1.15 us
    convert_element_type x1 -> x0, other arithmetic: 1.26 us -> none  [modulate(): (center / jnp.sqrt(spread + 1e-06) * (1.0 + scale) + shift).astype(jnp.bf...]
where the time goes in v3:
time: 77.5 us; the launch traced here: 76.4 us
  Pallas kernels  74.7 us (96%)
  local copies, waits for them, and re-layouts  1.15 us (1%)
    pallas_call x1, Pallas kernels, body(): pl.pallas_call(kernel, out_shape=pltpu.VMEM((steps_here, tok_here, width)...  74.7 us

profile of v3, /device:TPU:32, one launch (start us, length us, event | category | flops | bytes accessed | tf_op | source)
XLA Modules:
  0.0 76.4 jit_solution(10361438241979926456)
XLA Ops:
  0.0 0.5 multiply_exponential_fusion.freq_ref
  0.5 74.7 %shard_map.73 = f32[2,128,1536]{2,1,0:T(8,128)S(1)} custom-call(bf16[2,128,1536]{2,1,0:T(8,128)(2,1)} %x_ref.1, s32[17]{0:T(128)} %plan_ref.1, f32[1,128]{1,0:T(1,128)} %multiply_exponential_fusion.freq_ref, bf16[256,3072]{1,0:T(8,128)(2,1)} %mod_ref.1, bf16[48,4608]{1,0:T(8,128)(2,1)} %wqkv_ref.1, bf16[48,1536]{1,0:T(8,128)(2,1)} %wout_ref.1, ...), custom_call_target="tpu_custom_call" | custom-call | tf_op jit(solution)/shard_map/pallas_call | solution.py:514
  75.3 1.1 %copy.9 = f32[2,128,1536]{2,1,0:T(8,128)} copy(f32[2,128,1536]{2,1,0:T(8,128)S(1)} %shard_map.73) | data formatting | bytes 3145728

commit v4 on v3

--- a/solution.py
+++ b/solution.py
@@ -106,32 +106,43 @@
     def give(self, yh, off, i):
         pass
 
-    def whole(self, yh, c, other=False):
-        return self.buf.at[yh, :, c, :, self.rest if other else self.cols]
+    def whole(self, yh, k, other=False):
+        quarter = pl.ds(pl.multiple_of(lax.rem(self.x + k, XG) * self.span, HD), self.span)
+        return self.buf.at[yh, :, 1 - self.c if other else self.c, :, quarter]
 
     def swap(self):
-        self.push(self.whole(self.yh, self.c), 15, "x+")
-        self.push(self.whole(1 - self.yh, self.c), 16, "x-")
-        self.push(self.whole(self.yh, self.c), 17, "core")
-        self.push(self.whole(1 - self.yh, self.c), 18, "core")
+        for yh in range(2):
+            self.push(self.whole(yh, 0), 15 + yh, "x+")
+            self.push(self.whole(1 - yh, 0), 18 - yh, "x-")
+            self.push(self.whole(yh, 0), 21 + yh, "core")
+
+    def forward(self):
+        self.arrive(self.whole(0, 3), 15, "x+")
+        self.push(self.whole(0, 3), 19, "x+")
+        self.push(self.whole(0, 3), 23, "core")
+        self.arrive(self.whole(1, 1), 18, "x-")
+        self.push(self.whole(1, 1), 20, "x-")
+        self.push(self.whole(1, 1), 26, "core")
 
     def swapped(self):
-        self.arrive(self.whole(self.yh, self.c, True), 15, "x+")
-        self.push(self.whole(self.yh, self.c, True), 19, "core")
-        self.arrive(self.whole(1 - self.yh, self.c, True), 16, "x-")
-        self.push(self.whole(1 - self.yh, self.c, True), 20, "core")
+        self.arrive(self.whole(1, 3), 16, "x+")
+        self.push(self.whole(1, 3), 24, "core")
+        self.arrive(self.whole(0, 1), 17, "x-")
+        self.push(self.whole(0, 1), 25, "core")
+        self.arrive(self.whole(0, 2), 19, "x+")
+        self.push(self.whole(0, 2), 27, "core")
+        self.arrive(self.whole(1, 2), 20, "x-")
+        self.push(self.whole(1, 2), 28, "core")
 
     def shared(self):
-        c = 1 - self.c
-        self.arrive(self.whole(self.yh, c), 17, "core")
-        self.arrive(self.whole(1 - self.yh, c), 18, "core")
-        self.arrive(self.whole(self.yh, c, True), 19, "core")
-        self.arrive(self.whole(1 - self.yh, c, True), 20, "core")
+        for i, k in ((21, 0), (23, 3), (25, 1), (27, 2)):
+            for yh in range(2):
+                self.arrive(self.whole(yh, k, True), i + yh, "core")
 
 
 def kernel(
     x_ref, plan_ref, freq_ref, mod_ref, wqkv_ref, wout_ref, start_hbm, nb_ref, out_ref,
-    start_ref, own, modw, mods, hbuf, hnorm, wbuf, wo, kv0, kv1, kv2, kv3, abuf, tsend, trecv, sbuf, sall,
+    start_ref, own, modw, mods, hbuf, hnorm, wbuf, wo, kv0, kv1, kv2, kv3, abuf, tsend, trecv, sbuf, pass_on, sall,
     lsem, hs, hr, ws, wr, os, orecv, ks, kr, ts, tr, ss, sr,
 ):
     tm, tok = lax.axis_index("tm"), lax.axis_index("tok")
@@ -204,14 +215,9 @@
     cut = 2 * CW
     wfirst = Ring(wbuf, pl.ds(0, cut), ws, wr, 0, pos, peers)
     wlast = Ring(wbuf, pl.ds(cut, 3 * CW - cut), ws, wr, 31, pos, peers)
-    parity = lax.rem(x, 2)
-    span = width // 2
-
-    def wide(i):
-        return pl.ds(pl.multiple_of(i * span, HD), span)
-
-    oring = WideRing(wo, wide(parity), os, orecv, 0, pos, peers)
-    oring.rest = wide(1 - parity)
+    span = width // XG
+    oring = WideRing(wo, pl.ds(pl.multiple_of(x * span, HD), span), os, orecv, 0, pos, peers)
+    oring.x, oring.span = x, span
     wfirst.own()
     wlast.own()
     oring.own()
@@ -408,6 +414,10 @@
 
     keys_values(0)
     keys_values(1)
+    oring.collect(1)
+    oring.collect(2)
+    oring.collect(3)
+    oring.swap()
     keys_values(2)
     h_arrive(2)
     norm(3)
@@ -417,11 +427,8 @@
     project(1, 2, 3)
     project(2, 2, 3)
     project(3, 2, 3)
-    oring.collect(1)
-    oring.collect(2)
-    oring.collect(3)
-    oring.swap()
     attend(0)
+    oring.forward()
     attend(1)
     attend(2)
     attend(3)
@@ -431,6 +438,7 @@
         total = total + abuf[k]
     tsend[...] = total.astype(jnp.bfloat16)
     push(tsend, trecv, ts, tr, 0, lower)
+    oring.swapped()
     remote(trecv, trecv, ts, tr, 0, lower).wait_recv()
     run = jnp.where(yl > 0, trecv[...].astype(jnp.float32), 0.0)
     for k in range(2 * XG):
@@ -441,17 +449,32 @@
     def columns_of(src):
         return sall.at[:, :, pl.ds(pl.multiple_of(src * CW, HD), CW)]
 
-    for k in (1, 3, 2):
-        push(sbuf.at[pl.ds(2 * lax.rem(x + k, XG), 2)], columns_of(x), ss, sr, k - 1, at_x(k))
+    def piece(half, src):
+        return sall.at[half, :, pl.ds(pl.multiple_of(src * CW, HD), CW)]
+
+    far = lax.rem(x + 2, XG)
+    for half, k in ((0, 1), (1, 3)):
+        push(sbuf.at[2 * far + half], pass_on.at[half], ss, sr, 2 + half, at_x(k))
+    for k in (1, 3):
+        push(sbuf.at[pl.ds(2 * lax.rem(x + k, XG), 2)], columns_of(x), ss, sr, k // 2, at_x(k))
+    for half, k in ((0, 1), (1, 3)):
+        remote(pass_on.at[half], pass_on.at[half], ss, sr, 2 + half, at_x(k)).wait_recv()
+        push(
+            pass_on.at[half], piece(half, lax.rem(x + XG - k, XG)), ss, sr, 4 + half, at_x(k)
+        )
     keep = pltpu.make_async_copy(sbuf.at[pl.ds(2 * x, 2)], columns_of(x), lsem.at[4])
     keep.start()
-    oring.swapped()
     oring.shared()
     keep.wait()
 
     def s_arrive(k):
-        source = columns_of(lax.rem(x + XG - k, XG))
-        remote(source, source, ss, sr, k - 1, at_x(k)).wait_recv()
+        if k == 2:
+            for half, via in ((0, 1), (1, 3)):
+                source = piece(half, far)
+                remote(source, source, ss, sr, 4 + half, at_x(via)).wait_recv()
+        else:
+            source = columns_of(lax.rem(x + XG - k, XG))
+            remote(source, source, ss, sr, k // 2, at_x(k)).wait_recv()
 
     chunk = 256
 
@@ -530,14 +553,15 @@
             pltpu.VMEM((tok_here, CW), bf),
             pltpu.VMEM((tok_here, CW), bf),
             pltpu.VMEM((2 * XG, tok_here, CW), bf),
+            pltpu.VMEM((2, tok_here, CW), bf),
             pltpu.VMEM((steps_here, tok_here, width), bf),
             dma((8,)),
             dma((6,)), dma((6,)),
             dma((62,)), dma((62,)),
-            dma((21,)), dma((21,)),
+            dma((29,)), dma((29,)),
             dma((16,)), dma((16,)),
             dma((1,)), dma((1,)),
-            dma((3,)), dma((3,)),
+            dma((6,)), dma((6,)),
         ],
         compiler_params=pltpu.CompilerParams(
             collective_id=0, has_side_effects=True, vmem_limit_bytes=56 << 20

time: 77.5 us -> 75.4 us (0.973)
  Pallas kernels: 74.7 us -> 73.3 us
    pallas_call x1, Pallas kernels: 74.7 us -> 73.3 us  [body(): pl.pallas_call(kernel, out_shape=pltpu.VMEM((steps_here, tok_here, width)...]
where the time goes in v4:
time: 75.4 us; the launch traced here: 75 us
  Pallas kernels  73.3 us (97%)
  local copies, waits for them, and re-layouts  1.15 us (2%)
    pallas_call x1, Pallas kernels, body(): pl.pallas_call(kernel, out_shape=pltpu.VMEM((steps_here, tok_here, width)...  73.3 us

profile of v4, /device:TPU:32, one launch (start us, length us, event | category | flops | bytes accessed | tf_op | source)
XLA Modules:
  0.0 75.0 jit_solution(11655515910411999996)
XLA Ops:
  0.0 0.5 multiply_exponential_fusion.freq_ref
  0.5 73.3 %shard_map.73 = f32[2,128,1536]{2,1,0:T(8,128)S(1)} custom-call(bf16[2,128,1536]{2,1,0:T(8,128)(2,1)} %x_ref.1, s32[17]{0:T(128)} %plan_ref.1, f32[1,128]{1,0:T(1,128)} %multiply_exponential_fusion.freq_ref, bf16[256,3072]{1,0:T(8,128)(2,1)} %mod_ref.1, bf16[48,4608]{1,0:T(8,128)(2,1)} %wqkv_ref.1, bf16[48,1536]{1,0:T(8,128)(2,1)} %wout_ref.1, ...), custom_call_target="tpu_custom_call" | custom-call | tf_op jit(solution)/shard_map/pallas_call | solution.py:537
  73.9 1.1 %copy.9 = f32[2,128,1536]{2,1,0:T(8,128)} copy(f32[2,128,1536]{2,1,0:T(8,128)S(1)} %shard_map.73) | data formatting | bytes 3145728

commit v5 on v4

--- a/solution.py
+++ b/solution.py
@@ -142,7 +142,7 @@
 
 def kernel(
     x_ref, plan_ref, freq_ref, mod_ref, wqkv_ref, wout_ref, start_hbm, nb_ref, out_ref,
-    start_ref, own, modw, mods, hbuf, hnorm, wbuf, wo, kv0, kv1, kv2, kv3, abuf, tsend, trecv, sbuf, pass_on, sall,
+    start_ref, probs, gains, own, modw, mods, hbuf, hnorm, wbuf, wo, qs, k0, k1, k2, k3, v0, v1, v2, v3, abuf, tsend, trecv, sbuf, pass_on, sall,
     lsem, hs, hr, ws, wr, os, orecv, ks, kr, ts, tr, ss, sr,
 ):
     tm, tok = lax.axis_index("tm"), lax.axis_index("tok")
@@ -322,41 +322,40 @@
     oring.relay(3)
     wfirst.shared()
 
-    kvs = (kv0, kv1, kv2, kv3)
-
-    def project(group, first, last):
-        kv = kvs[group]
-
-        def one(j, carry):
-            column = pl.multiple_of(j * CW, HD)
-            left = hnorm[group]
-            right = wbuf[:, :, :, :, pl.ds(column, CW)].reshape(width, CW)
-            part = jnp.dot(left, right, preferred_element_type=jnp.float32)
-            pieces = []
-            for head in range(HL):
-                piece = part[:, head * HD : (head + 1) * HD]
-                norm = lax.rsqrt(jnp.mean(piece * piece, -1, keepdims=True) + 1e-06)
-                pieces.append(piece * jnp.where(j == 1, 1.0, norm))
-            done = jnp.concatenate(pieces, axis=1).astype(jnp.bfloat16)
-            for half in range(2):
-                for tile in range(2):
-                    row = half * part_rows + tile * TILE
-                    kv[2 + tile, j, half] = done[row : row + TILE]
-            return carry
-
-        lax.fori_loop(first, last, one, 0)
+    ks_of, vs_of = (k0, k1, k2, k3), (v0, v1, v2, v3)
+
+    def project(group, j):
+        left = hnorm[group]
+        right = wbuf[:, :, :, :, j * CW : (j + 1) * CW].reshape(width, CW)
+        part = jnp.dot(left, right, preferred_element_type=jnp.float32)
+        pieces = []
+        for head in range(HL):
+            piece = part[:, head * HD : (head + 1) * HD]
+            if j != 1:
+                piece = piece * lax.rsqrt(jnp.mean(piece * piece, -1, keepdims=True) + 1e-06)
+            pieces.append(piece)
+        done = jnp.concatenate(pieces, axis=1).astype(jnp.bfloat16)
+        for half in range(2):
+            for tile in range(2):
+                row = half * part_rows + tile * TILE
+                piece = done[row : row + TILE]
+                if j == 2:
+                    qs[group, tile, half] = piece
+                else:
+                    (ks_of, vs_of)[j][group][2 + tile, half] = piece
 
     def halo(group, j):
-        mine = kvs[group].at[2:4, j]
+        ref = (ks_of, vs_of)[j][group]
+        mine = ref.at[2:4]
         i = 4 * group + 2 * j
         return (
-            remote(mine, kvs[group].at[0:2, j], ks, kr, i, at_tok(1)),
-            remote(mine, kvs[group].at[4:6, j], ks, kr, i + 1, at_tok(-1)),
+            remote(mine, ref.at[0:2], ks, kr, i, at_tok(1)),
+            remote(mine, ref.at[4:6], ks, kr, i + 1, at_tok(-1)),
         )
 
     def keys_values(group):
         for j in range(2):
-            project(group, j, j + 1)
+            project(group, j)
             ahead, behind = halo(group, j)
 
             @pl.when(tok < ntok - 1)
@@ -368,31 +367,28 @@
                 behind.start()
 
     def attend(group):
-        kv = kvs[group]
         copies = [halo(group, j) for j in range(2)]
 
-        @pl.when(tok > 0)
-        def _():
-            for ahead, _ in copies:
-                ahead.wait_recv()
-
-        @pl.when(tok < ntok - 1)
-        def _():
-            for _, behind in copies:
-                behind.wait_recv()
-
-
-        def one(i, carry):
+        def arrived(j):
+            @pl.when(tok > 0)
+            def _():
+                copies[j][0].wait_recv()
+
+            @pl.when(tok < ntok - 1)
+            def _():
+                copies[j][1].wait_recv()
+
+        def near(tile):
+            return [
+                jnp.clip(nb_ref[tile, n] - (2 * tok - 2), 0, 5) for n in range(nb_ref.shape[1])
+            ]
+
+        def weigh(i, carry):
             half, tile = lax.div(i, 2), lax.rem(i, 2)
             when = timestep(group, half)
             step = time_of(when) - time_of(when + 1)
-            near = [
-                jnp.clip(nb_ref[tile, n] - (2 * tok - 2), 0, 5) for n in range(nb_ref.shape[1])
-            ]
-            query = kv[2 + tile, 2, half]
-            keys = jnp.concatenate([kv[n, 0, half] for n in near], axis=0)
-            values = jnp.concatenate([kv[n, 1, half] for n in near], axis=0)
-            outs = []
+            query = qs[group, tile, half]
+            keys = jnp.concatenate([ks_of[group][n, half] for n in near(tile)], axis=0)
             for head in range(HL):
                 cols = slice(head * HD, (head + 1) * HD)
                 score = lax.dot_general(
@@ -401,16 +397,28 @@
                 ) * (1.0 / math.sqrt(HD))
                 expo = jnp.exp(score)
                 total = jnp.sum(expo, -1, keepdims=True)
+                probs[i, head] = expo.astype(jnp.bfloat16)
+                gains[i, head] = step / total
+            return carry
+
+        def mix(i, carry):
+            half, tile = lax.div(i, 2), lax.rem(i, 2)
+            values = jnp.concatenate([vs_of[group][n, half] for n in near(tile)], axis=0)
+            outs = []
+            for head in range(HL):
                 mixed = jnp.dot(
-                    expo.astype(jnp.bfloat16), values[:, cols], preferred_element_type=jnp.float32
+                    probs[i, head], values[:, head * HD : (head + 1) * HD],
+                    preferred_element_type=jnp.float32,
                 )
-                outs.append(mixed * (step / total))
-            abuf[when, pl.ds(pl.multiple_of(tile * TILE, TILE), TILE), :] = jnp.concatenate(
-                outs, axis=1
-            )
+                outs.append(mixed * gains[i, head])
+            rows_at = pl.ds(pl.multiple_of(tile * TILE, TILE), TILE)
+            abuf[timestep(group, half), rows_at, :] = jnp.concatenate(outs, axis=1)
             return carry
 
-        lax.fori_loop(0, 4, one, 0, unroll=4)
+        arrived(0)
+        lax.fori_loop(0, 4, weigh, 0, unroll=4)
+        arrived(1)
+        lax.fori_loop(0, 4, mix, 0, unroll=4)
 
     keys_values(0)
     keys_values(1)
@@ -423,13 +431,13 @@
     norm(3)
     keys_values(3)
     wlast.shared()
-    project(0, 2, 3)
-    project(1, 2, 3)
-    project(2, 2, 3)
-    project(3, 2, 3)
+    project(0, 2)
+    project(1, 2)
+    project(2, 2)
+    project(3, 2)
     attend(0)
+    attend(1)
     oring.forward()
-    attend(1)
     attend(2)
     attend(3)
 
@@ -438,7 +446,6 @@
         total = total + abuf[k]
     tsend[...] = total.astype(jnp.bfloat16)
     push(tsend, trecv, ts, tr, 0, lower)
-    oring.swapped()
     remote(trecv, trecv, ts, tr, 0, lower).wait_recv()
     run = jnp.where(yl > 0, trecv[...].astype(jnp.float32), 0.0)
     for k in range(2 * XG):
@@ -457,6 +464,7 @@
         push(sbuf.at[2 * far + half], pass_on.at[half], ss, sr, 2 + half, at_x(k))
     for k in (1, 3):
         push(sbuf.at[pl.ds(2 * lax.rem(x + k, XG), 2)], columns_of(x), ss, sr, k // 2, at_x(k))
+    oring.swapped()
     for half, k in ((0, 1), (1, 3)):
         remote(pass_on.at[half], pass_on.at[half], ss, sr, 2 + half, at_x(k)).wait_recv()
         push(
@@ -529,7 +537,7 @@
     half = mod_weight.shape[0] // 2
     freqs = jnp.exp(-math.log(10000.0) * jnp.arange(half, dtype=jnp.float32) / half)[None]
     bf, f32 = jnp.bfloat16, jnp.float32
-    kv = pltpu.VMEM((6, 3, steps_here, TILE, CW), bf)
+    kv = pltpu.VMEM((6, steps_here, TILE, CW), bf)
     dma = pltpu.SemaphoreType.DMA
     vmem = pl.BlockSpec(memory_space=pltpu.VMEM)
     smem = pl.BlockSpec(memory_space=pltpu.SMEM)
@@ -541,6 +549,8 @@
         out_specs=vmem,
         scratch_shapes=[
             pltpu.VMEM((tok_here, width), bf),
+            pltpu.VMEM((4, HL, TILE, 3 * TILE), bf),
+            pltpu.VMEM((4, HL, TILE, HD), f32),
             pltpu.VMEM((steps_here, tok_here, width), bf),
             pltpu.VMEM(mod_weight.shape, bf),
             pltpu.VMEM((2 * XG, 2 * width), f32),
@@ -548,7 +558,8 @@
             pltpu.VMEM((4, rows, width), bf),
             pltpu.VMEM((2, ZG, 2, w_qkv.shape[0], 3 * CW), bf),
             pltpu.VMEM((2, ZG, 2, w_out.shape[0], width), bf),
-            kv, kv, kv, kv,
+            pltpu.VMEM((4, 2, steps_here, TILE, CW), bf),
+            kv, kv, kv, kv, kv, kv, kv, kv,
             pltpu.VMEM((2 * XG, tok_here, CW), f32),
             pltpu.VMEM((tok_here, CW), bf),
             pltpu.VMEM((tok_here, CW), bf),

time: 75.4 us -> 74.1 us (0.983)
  Pallas kernels: 73.3 us -> 71.4 us
    pallas_call x1, Pallas kernels: 73.3 us -> 71.4 us  [body(): pl.pallas_call(kernel, out_shape=pltpu.VMEM((steps_here, tok_here, width)...]
where the time goes in v5:
time: 74.1 us; the launch traced here: 73.1 us
  Pallas kernels  71.4 us (96%)
  local copies, waits for them, and re-layouts  1.15 us (2%)
    pallas_call x1, Pallas kernels, body(): pl.pallas_call(kernel, out_shape=pltpu.VMEM((steps_here, tok_here, width)...  71.4 us

profile of v5, /device:TPU:32, one launch (start us, length us, event | category | flops | bytes accessed | tf_op | source)
XLA Modules:
  0.0 73.1 jit_solution(2612980906645039604)
XLA Ops:
  0.0 0.5 multiply_exponential_fusion.freq_ref
  0.5 71.4 %shard_map.73 = f32[2,128,1536]{2,1,0:T(8,128)S(1)} custom-call(bf16[2,128,1536]{2,1,0:T(8,128)(2,1)} %x_ref.1, s32[17]{0:T(128)} %plan_ref.1, f32[1,128]{1,0:T(1,128)} %multiply_exponential_fusion.freq_ref, bf16[256,3072]{1,0:T(8,128)(2,1)} %mod_ref.1, bf16[48,4608]{1,0:T(8,128)(2,1)} %wqkv_ref.1, bf16[48,1536]{1,0:T(8,128)(2,1)} %wout_ref.1, ...), custom_call_target="tpu_custom_call" | custom-call | tf_op jit(solution)/shard_map/pallas_call | solution.py:545
  72.0 1.1 %copy.9 = f32[2,128,1536]{2,1,0:T(8,128)} copy(f32[2,128,1536]{2,1,0:T(8,128)S(1)} %shard_map.73) | data formatting | bytes 3145728

commit v6 on v5

--- a/solution.py
+++ b/solution.py
@@ -486,11 +486,11 @@
 
     chunk = 256
 
-    def finish(near):
+    def finish(hops):
         def one(i, carry):
             column = pl.ds(pl.multiple_of(i * chunk, chunk), chunk)
             before = 0.0
-            for k in (0, 1, 3) if near else (2,):
+            for k in hops:
                 src = lax.rem(x + k, XG)
                 left = sall[:, :, pl.ds(pl.multiple_of(src * CW, HD), CW)].reshape(rows, CW)
                 part = pl.ds(lax.rem(src, 2) * (ZG // 2), ZG // 2)
@@ -498,20 +498,21 @@
                 before = before + jnp.dot(left, right, preferred_element_type=jnp.float32)
             for half in range(2):
                 done = before[half * part_rows : (half + 1) * part_rows]
-                if near:
+                if 0 in hops:
                     first = start_ref[:, column].astype(jnp.float32)
                 else:
                     first = out_ref[half, :, column]
                 out_ref[half, :, column] = first - done
             return carry
 
-        lax.fori_loop(0, width // chunk, one, 0)
-
+        lax.fori_loop(0, width // chunk, one, 0, unroll=2)
+
+    finish((0,))
     s_arrive(1)
     s_arrive(3)
-    finish(True)
+    finish((1, 3))
     s_arrive(2)
-    finish(False)
+    finish((2,))
     wfirst.finish()
     wlast.finish()
     oring.finish()

time: 74.1 us -> 73.3 us (0.989)
  Pallas kernels: 71.4 us -> 70.3 us
    pallas_call x1, Pallas kernels: 71.4 us -> 70.3 us  [body(): pl.pallas_call(kernel, out_shape=pltpu.VMEM((steps_here, tok_here, width)...]
where the time goes in v6:
time: 73.3 us; the launch traced here: 71.9 us
  Pallas kernels  70.3 us (96%)
  local copies, waits for them, and re-layouts  1.15 us (2%)
    pallas_call x1, Pallas kernels, body(): pl.pallas_call(kernel, out_shape=pltpu.VMEM((steps_here, tok_here, width)...  70.3 us

profile of v6, /device:TPU:32, one launch (start us, length us, event | category | flops | bytes accessed | tf_op | source)
XLA Modules:
  0.0 71.9 jit_solution(4244434266810771373)
XLA Ops:
  0.0 0.5 multiply_exponential_fusion.freq_ref
  0.5 70.3 %shard_map.73 = f32[2,128,1536]{2,1,0:T(8,128)S(1)} custom-call(bf16[2,128,1536]{2,1,0:T(8,128)(2,1)} %x_ref.1, s32[17]{0:T(128)} %plan_ref.1, f32[1,128]{1,0:T(1,128)} %multiply_exponential_fusion.freq_ref, bf16[256,3072]{1,0:T(8,128)(2,1)} %mod_ref.1, bf16[48,4608]{1,0:T(8,128)(2,1)} %wqkv_ref.1, bf16[48,1536]{1,0:T(8,128)(2,1)} %wout_ref.1, ...), custom_call_target="tpu_custom_call" | custom-call | tf_op jit(solution)/shard_map/pallas_call | solution.py:546
  70.8 1.1 %copy.9 = f32[2,128,1536]{2,1,0:T(8,128)} copy(f32[2,128,1536]{2,1,0:T(8,128)S(1)} %shard_map.73) | data formatting | bytes 3145728
